TPU v7x, 128 devices: a whole 4x4x4 slice. The times are simulated.
128 devices in a mesh: rows: 32 (over z, y, core), fib: 4 (over x).
Axes of the slice: x: 4, y: 4, z: 4, core: 2. Of those that a mesh axis runs over, the one named last changes fastest.
Arguments:
- frames: bfloat16 [20, 4096, 4096], P('fib', 'rows'), may hold values from 0 to 2
- amplitude: float32 [20, 512], P('fib'), may hold values from 0.5 to 2
- line_start: int32 [20, 24], P('fib'), may hold values from 0 to 4088
- bundle_width: float32 [20], replicated, may hold values from 0.8 to 1.6
- fiber_bundle: int32 [512], replicated, may hold values from 0 to 19
- trace_coef: float32 [512, 11], P(('rows', 'fib')), may hold values from -1 to 1
- width_coef: float32 [512, 11], P(('rows', 'fib')), may hold values from -0.15 to 0.15
Outputs:
- trace_fit: float32 [512, 11], P(('rows', 'fib'))
- width_fit: float32 [512, 11], P(('rows', 'fib'))
- residual: bfloat16 [20, 4096, 4096], P('fib', 'rows')
All inputs are finite; a program needn't handle non-finite values.
Results may differ from a plain program's by a relative error of at most 0.001.
Values sent between devices are 32-bit elements; how exact they have to be, the bound alone decides.
A program may use at most 128 MiB of HBM per device.

v0:
```python
import jax
import jax.numpy as jnp
from jax import lax
from jax.sharding import Mesh
from jax.sharding import PartitionSpec as P

K = 11
PIX = 8
WIN = 8
ITERS = 3
ROWS = ("rows_0", "rows_1", "rows_2")
ROWS_FIB = ("rows_0", "rows_1", "rows_2", "fib")


HIGH = lax.Precision.HIGHEST


def sent_together(arrays, axis, dim, along):
    both = jnp.concatenate(arrays, axis=along)
    result, at, finished = (lax.all_gather(both, axis, axis=dim, tiled=True), 0, [])
    for a in arrays:
        finished.append(lax.slice_in_dim(result, at, at + a.shape[along], axis=along))
        at += a.shape[along]
    return tuple(finished)


def in_blocks(x, dim, peers):
    before, after = (x.shape[:dim], x.shape[dim + 1 :])
    return jnp.moveaxis(x.reshape(*before, peers, -1, *after), dim, 0)


def sum_at_owner(x, axis, dim):
    blocks = in_blocks(x, dim, lax.axis_size(axis))
    arrived = lax.all_to_all(blocks, axis, split_axis=0, concat_axis=0, tiled=True)
    return arrived.sum(axis=0)


def sum_in_two_steps(x, axes, dim):
    far, near = axes
    blocks = in_blocks(x, dim, lax.axis_size(far))
    nearer = sum_at_owner(blocks, near, dim + 1)
    arrived = lax.all_to_all(nearer, far, split_axis=0, concat_axis=0, tiled=True)
    return arrived.sum(axis=0)


def side_by_side(arrays, axis, dim, along):
    both = jnp.concatenate(arrays, axis=along)
    result, at, finished = (sum_in_two_steps(both, axis, dim), 0, [])
    for a in arrays:
        finished.append(lax.slice_in_dim(result, at, at + a.shape[along], axis=along))
        at += a.shape[along]
    return tuple(finished)


def from_everyone(x, axis):
    peers = lax.axis_size(axis)
    return lax.all_to_all(jnp.broadcast_to(x[None], (peers, *x.shape)), axis, 0, 0, tiled=True)


def laid_out(blocks, dim):
    blocks = jnp.moveaxis(blocks, 0, dim)
    shape = blocks.shape
    return blocks.reshape(*shape[:dim], shape[dim] * shape[dim + 1], *shape[dim + 2 :])


def whole_of(x, axes, dim):
    far, near = axes
    blocks = from_everyone(from_everyone(x, far), near)
    return laid_out(blocks.swapaxes(0, 1).reshape(-1, *x.shape), dim)


def legendre_upto(first, count, total, degree_count):
    rowpos = (first + jnp.arange(count, dtype=jnp.int32)).astype(jnp.float32)
    tvals = (2.0 * rowpos + 1.0) / total - 1.0
    polys = [jnp.ones_like(tvals), tvals]
    for order in range(1, degree_count - 1):
        polys.append(
            ((2 * order + 1) * tvals * polys[order] - order * polys[order - 1]) / (order + 1)
        )
    return jnp.stack(polys[:degree_count], axis=1)


def legendre_table(first, count, total):
    return legendre_upto(first, count, total, K)


def adams_factor(order):
    value = 1.0
    for index in range(1, order + 1):
        value = value * (2.0 * index - 1.0) / index
    return value


def product_table():
    moment_count = 2 * K - 1
    entries = [[0.0] * (K * K) for index in range(moment_count)]
    for first_deg in range(K):
        for second_deg in range(K):
            for inner_m in range(min(first_deg, second_deg) + 1):
                target = first_deg + second_deg - 2 * inner_m
                weight = (
                    adams_factor(inner_m)
                    * adams_factor(first_deg - inner_m)
                    * adams_factor(second_deg - inner_m)
                )
                weight = weight / adams_factor(first_deg + second_deg - inner_m)
                weight = (
                    weight * (2.0 * target + 1.0) / (2.0 * (first_deg + second_deg - inner_m) + 1.0)
                )
                entries[target][first_deg * K + second_deg] += weight
    return jnp.asarray(entries, dtype=jnp.float32)


def lit_rows(line_start, first, count):
    rowid = first + jnp.arange(count, dtype=jnp.int32)
    low = line_start[:, None, :]
    inside = (rowid[None, :, None] >= low) & (rowid[None, :, None] < low + WIN)
    return jnp.any(inside, axis=2).astype(jnp.float32)


def profile_cols(trace, width, bundle_width, fiber_bundle, ptab):
    onehot = (
        fiber_bundle[:, None] == jnp.arange(bundle_width.shape[0], dtype=jnp.int32)[None, :]
    ).astype(jnp.float32)
    base = jnp.dot(onehot, bundle_width, precision=HIGH)
    centre = jnp.dot(ptab, trace.T, precision=HIGH)
    spread = base[None, :] * jnp.exp(jnp.dot(ptab, width.T, precision=HIGH))
    offsets = jnp.arange(PIX, dtype=jnp.float32) - (PIX - 1) / 2.0
    fibers = trace.shape[0]
    return (
        jnp.repeat(centre, PIX, axis=1),
        jnp.repeat(spread, PIX, axis=1),
        jnp.tile(offsets, fibers),
    )


def lamp_model(lit_row, amp_row, centre, spread, offsets):
    scaled = (offsets[None, :] - centre) / spread
    shape = lit_row[:, None] * amp_row[None, :] * jnp.exp(-0.5 * scaled * scaled)
    return (shape, scaled)


def accumulate(frames, lit, amp_cols, centre, spread, offsets):

    def accumulate_one_lamp(carry, item):
        frame, lit_row, amp_row = item
        shape, scaled = lamp_model(lit_row, amp_row, centre, spread, offsets)
        resid = frame.astype(jnp.float32) - shape
        slope = shape * scaled / spread
        widen = shape * scaled * scaled
        return (
            (
                carry[0] + slope * slope,
                carry[1] + slope * widen,
                carry[2] + widen * widen,
                carry[3] + resid * slope,
                carry[4] + resid * widen,
            ),
            None,
        )

    zeros = jnp.zeros(centre.shape, jnp.float32)
    sums, _ = lax.scan(
        accumulate_one_lamp, (zeros, zeros, zeros, zeros, zeros), (frames, lit, amp_cols)
    )
    rows_here, cols = centre.shape
    return tuple((item.reshape(rows_here, cols // PIX, PIX).sum(axis=2) for item in sums))


def assemble(nxx, nxs, nss):
    fibers = nxx.shape[0]
    upper = jnp.concatenate([nxx, nxs], axis=2)
    lower = jnp.concatenate([jnp.swapaxes(nxs, 1, 2), nss], axis=2)
    return jnp.concatenate([upper, lower], axis=1).reshape(fibers, 4 * K * K)


def gradient_cols(sums, ptab):
    return jnp.concatenate(
        [jnp.dot(sums[3].T, ptab, precision=HIGH), jnp.dot(sums[4].T, ptab, precision=HIGH)], axis=1
    )


def from_moments(moment_xx, moment_xs, moment_ss, link):
    fibers = moment_xx.shape[0]
    nxx = jnp.dot(moment_xx, link, precision=HIGH).reshape(fibers, K, K)
    nxs = jnp.dot(moment_xs, link, precision=HIGH).reshape(fibers, K, K)
    nss = jnp.dot(moment_ss, link, precision=HIGH).reshape(fibers, K, K)
    return assemble(nxx, nxs, nss)


def solve_step(normal, grad, trace, width):
    fibers = normal.shape[0]
    matrix = normal.reshape(fibers, 2 * K, 2 * K)
    diag_vals = jnp.diagonal(matrix, axis1=1, axis2=2)
    eye_mat = jnp.eye(2 * K, dtype=jnp.float32)
    matrix = matrix + (0.5 * diag_vals + 1.0)[:, :, None] * eye_mat[None, :, :]
    factor = jnp.linalg.cholesky(matrix)
    inner = jax.scipy.linalg.solve_triangular(factor, grad[:, :, None], lower=True)
    update = jax.scipy.linalg.solve_triangular(factor, inner, lower=True, trans=1)[:, :, 0]
    return (trace + update[:, :K], width + update[:, K:])


def residual_image(frames, lit, amp_cols, centre, spread, offsets):

    def residual_one_lamp(item):
        frame, lit_row, amp_row = item
        shape, scaled = lamp_model(lit_row, amp_row, centre, spread, offsets)
        return (frame.astype(jnp.float32) - shape).astype(jnp.bfloat16)

    return lax.map(residual_one_lamp, (frames, lit, amp_cols))


def body(frames, amplitude, line_start, bundle_width, fiber_bundle, trace_coef, width_coef):
    rows_here = frames.shape[1]
    nrow = rows_here * lax.axis_size(ROWS)
    first = lax.axis_index(ROWS) * rows_here
    ptab = legendre_table(first, rows_here, nrow)
    lit = lit_rows(line_start, first, rows_here)
    amp_cols = jnp.repeat(amplitude, PIX, axis=1)
    trace_all, width_all = sent_together((trace_coef, width_coef), ROWS_FIB, 0, 1)
    trace_own, width_own = (trace_coef, width_coef)
    wide_tab = legendre_upto(first, rows_here, nrow, 2 * K - 1)
    link = product_table()
    for step in range(ITERS):
        centre, spread, offsets = profile_cols(
            trace_all, width_all, bundle_width, fiber_bundle, ptab
        )
        sums = accumulate(frames, lit, amp_cols, centre, spread, offsets)
        moment_xx = jnp.dot(sums[0].T, wide_tab, precision=HIGH)
        moment_xs = jnp.dot(sums[1].T, wide_tab, precision=HIGH)
        moment_ss = jnp.dot(sums[2].T, wide_tab, precision=HIGH)
        grad = gradient_cols(sums, ptab)
        own_xx, own_xs, own_ss, grad_own = side_by_side(
            (moment_xx, moment_xs, moment_ss, grad), (("rows_0", "rows_1"), ("rows_2", "fib")), 0, 1
        )
        normal_own = from_moments(own_xx, own_xs, own_ss, link)
        trace_own, width_own = solve_step(normal_own, grad_own, trace_own, width_own)
        trace_all, width_all = (
            whole_of(trace_own, (("rows_0", "rows_1"), ("rows_2", "fib")), 0),
            whole_of(width_own, (("rows_0", "rows_1"), ("rows_2", "fib")), 0),
        )
    centre, spread, offsets = profile_cols(trace_all, width_all, bundle_width, fiber_bundle, ptab)
    return (trace_own, width_own, residual_image(frames, lit, amp_cols, centre, spread, offsets))


def solution(mesh):
    finer = Mesh(
        mesh.devices.reshape(4, 4, 2, mesh.shape["fib"]), ("rows_0", "rows_1", "rows_2", "fib")
    )
    placed = (
        P("fib", ROWS, None),
        P("fib", None),
        P("fib", None),
        P(),
        P(),
        P(ROWS_FIB, None),
        P(ROWS_FIB, None),
    )
    return jax.shard_map(
        body,
        mesh=finer,
        in_specs=placed,
        out_specs=(P(ROWS_FIB, None), P(ROWS_FIB, None), P("fib", ROWS, None)),
        check_vma=False,
    )
```

profile of v0, /device:TPU:1, one launch (start us, length us, event | category | flops | bytes accessed | tf_op | source)
XLA Modules:
  0.0 514.3 jit_solution(12577817375139874748)
XLA Ops:
  1.9 63.3 %all-gather = f32[128,4,22]{2,1,0:T(4,128)S(1)} all-gather(f32[1,4,22]{2,1,0:T(4,128)S(1)} %maximum_bitcast_fusion), channel_id=1, replica_groups=mesh['rows_0'=4,'rows_1'=4,'rows_2'=2,'fib'=4] {'rows_0','rows_1','rows_..., dimensions={0}, use_global_device_ids=true | all-gather | bytes 45408 | tf_op jit(solution)/shard_map/all_gather | solution.py:20
  68.9 7.8 %copy.304 = bf16[5,128,4096]{1,2,0:T(8,128)(2,1)} copy(bf16[5,128,4096]{2,1,0:T(8,128)(2,1)} %param.21) | data formatting | bytes 10485760
  80.1 47.4 %while.69 = (s32[]{:T(128)}, f32[128,4096]{0,1:T(8,128)S(1)}, f32[128,4096]{0,1:T(8,128)}, f32[128,4096]{0,1:T(8,128)}, f32[128,4096]{0,1:T(8,128)}, /*index=5*/...) while((s32[]{:T(128)}, f32[128,4096]{0,1:T(8,128)S(1)}, ...), condition=%wide.region_2.3_spmd.clone, body=%wide.region_1.2_spmd.clone.sunk | while | flops 13631491 | bytes 22660792 | solution.py:163
  80.4 8.1 %select_add_fusion.18 = (f32[128,4096]{0,1:T(8,128)}, f32[128,4096]{0,1:T(8,128)}, f32[128,4096]{0,1:T(8,128)}, f32[128,4096]{0,1:T(8,128)}, f32[128,4096]{0,1:T(8,128)S(1)}) fusion(f32[128,4096]{0,1:T(8,128)} %get-tuple-element.1157, pred[]{:T(512)S(6)} %compare.17, f32[128,512]{0,1:T(8,128)S(1)} %get-tuple-element.1177, ...), kind=kLoop, calls=%fused_computation.33.clone.1 | loop fusion | flops 13631488 | bytes 22577668 | tf_op jit(solution)/shard_map/while/body/eval_jaxpr/add | solution.py:157
  88.7 9.5 %select_add_fusion.18 = (f32[128,4096]{0,1:T(8,128)}, f32[128,4096]{0,1:T(8,128)}, f32[128,4096]{0,1:T(8,128)}, f32[128,4096]{0,1:T(8,128)}, f32[128,4096]{0,1:T(8,128)S(1)}) fusion(f32[128,4096]{0,1:T(8,128)} %get-tuple-element.1157, pred[]{:T(512)S(6)} %compare.17, f32[128,512]{0,1:T(8,128)S(1)} %get-tuple-element.1177, ...), kind=kLoop, calls=%fused_computation.33.clone.1 | loop fusion | flops 13631488 | bytes 22577668 | tf_op jit(solution)/shard_map/while/body/eval_jaxpr/add | solution.py:157
  98.5 9.5 %select_add_fusion.18 = (f32[128,4096]{0,1:T(8,128)}, f32[128,4096]{0,1:T(8,128)}, f32[128,4096]{0,1:T(8,128)}, f32[128,4096]{0,1:T(8,128)}, f32[128,4096]{0,1:T(8,128)S(1)}) fusion(f32[128,4096]{0,1:T(8,128)} %get-tuple-element.1157, pred[]{:T(512)S(6)} %compare.17, f32[128,512]{0,1:T(8,128)S(1)} %get-tuple-element.1177, ...), kind=kLoop, calls=%fused_computation.33.clone.1 | loop fusion | flops 13631488 | bytes 22577668 | tf_op jit(solution)/shard_map/while/body/eval_jaxpr/add | solution.py:157
  108.2 9.5 %select_add_fusion.18 = (f32[128,4096]{0,1:T(8,128)}, f32[128,4096]{0,1:T(8,128)}, f32[128,4096]{0,1:T(8,128)}, f32[128,4096]{0,1:T(8,128)}, f32[128,4096]{0,1:T(8,128)S(1)}) fusion(f32[128,4096]{0,1:T(8,128)} %get-tuple-element.1157, pred[]{:T(512)S(6)} %compare.17, f32[128,512]{0,1:T(8,128)S(1)} %get-tuple-element.1177, ...), kind=kLoop, calls=%fused_computation.33.clone.1 | loop fusion | flops 13631488 | bytes 22577668 | tf_op jit(solution)/shard_map/while/body/eval_jaxpr/add | solution.py:157
  118.0 9.5 %select_add_fusion.18 = (f32[128,4096]{0,1:T(8,128)}, f32[128,4096]{0,1:T(8,128)}, f32[128,4096]{0,1:T(8,128)}, f32[128,4096]{0,1:T(8,128)}, f32[128,4096]{0,1:T(8,128)S(1)}) fusion(f32[128,4096]{0,1:T(8,128)} %get-tuple-element.1157, pred[]{:T(512)S(6)} %compare.17, f32[128,512]{0,1:T(8,128)S(1)} %get-tuple-element.1177, ...), kind=kLoop, calls=%fused_computation.33.clone.1 | loop fusion | flops 13631488 | bytes 22577668 | tf_op jit(solution)/shard_map/while/body/eval_jaxpr/add | solution.py:157
  136.8 4.0 all-to-all-start
  140.9 6.5 %all-to-all-done = f32[8,16,4,85]{3,2,1,0:T(4,128)S(1)} async-done(((f32[8,16,4,85]{3,2,1,0:T(4,128)}), f32[8,16,4,85]{3,2,1,0:T(4,128)S(1)}, u32[]{:S(2)}, u32[]{:S(2)}) %all-to-all-start) | async-done | bytes 174112 | tf_op jit(solution)/shard_map/all_to_all | solution.py:34
  148.1 4.6 all-to-all-start.1
  152.8 6.4 %all-to-all-done.1 = f32[16,4,85]{2,1,0:T(4,128)S(1)} async-done(((f32[16,4,85]{2,1,0:T(4,128)}), f32[16,4,85]{2,1,0:T(4,128)S(1)}, u32[]{:S(2)}, u32[]{:S(2)}) %all-to-all-start.1) | async-done | bytes 21792 | tf_op jit(solution)/shard_map/all_to_all | solution.py:42
  161.8 8.1 %custom-call.36 = f32[4,22,22]{2,1,0:T(8,128)S(1)} custom-call(f32[4,22,22]{2,1,0:T(8,128)S(1)} %fusion.64), custom_call_target="Cholesky" | custom-call | tf_op jit(solution)/shard_map/jit(cholesky)/cholesky | solution.py:197
  170.1 6.8 %custom-call.38 = f32[4,1,22,22]{2,3,1,0:T(8,128)S(1)} custom-call(f32[4,1,22,22]{3,2,1,0:T(8,128)S(1)} %select_bitcast_fusion.2), custom_call_target="InvertDiagBlocksLowerTriangular" | custom-call | tf_op jit(solution)/shard_map/jit(_solve_triangular)/vmap()/triangular_solve | solution.py:199
  178.0 3.5 all-to-all-start.4
  181.5 6.3 %all-to-all-done.4 = f32[16,4,11]{2,1,0:T(4,128)S(1)} async-done(((f32[16,4,11]{2,1,0:T(4,128)}), f32[16,4,11]{2,1,0:T(4,128)S(1)}, u32[]{:S(2)}, u32[]{:S(2)}) %all-to-all-start.4) | async-done | bytes 2848 | tf_op jit(solution)/shard_map/all_to_all | solution.py:57
  188.5 3.5 all-to-all-start.2
  192.8 5.5 %all-to-all-done.2 = f32[16,4,11]{2,1,0:T(4,128)S(1)} async-done(((f32[16,4,11]{2,1,0:T(4,128)}), f32[16,4,11]{2,1,0:T(4,128)S(1)}, u32[]{:S(2)}, u32[]{:S(2)}) %all-to-all-start.2) | async-done | bytes 2848 | tf_op jit(solution)/shard_map/all_to_all | solution.py:57
  198.3 7.3 %all-to-all-start.5 = ((f32[8,1,704]{2,1,0:T(1,128)}), f32[8,1,704]{2,1,0:T(1,128)S(1)}, u32[]{:S(2)}, u32[]{:S(2)}) async-start(f32[8,1,704]{2,1,0:T(1,128)} %reshape.737), calls=%async_computation.5 | async-start | bytes 49152 | tf_op jit(solution)/shard_map/all_to_all | solution.py:57
  206.6 4.0 all-to-all-done.5
  210.5 3.6 all-to-all-start.3
  216.5 2.6 all-to-all-done.3
  220.7 47.4 %while.70 = (s32[]{:T(128)}, f32[128,4096]{0,1:T(8,128)S(1)}, f32[128,4096]{0,1:T(8,128)}, f32[128,4096]{0,1:T(8,128)}, f32[128,4096]{0,1:T(8,128)}, /*index=5*/...) while((s32[]{:T(128)}, f32[128,4096]{0,1:T(8,128)S(1)}, ...), condition=%wide.region_13.17_spmd.clone, body=%wide.region_12.16_spmd.clone.sunk | while | flops 13631491 | bytes 22660792 | solution.py:163
  220.9 8.1 %select_add_fusion.19 = (f32[128,4096]{0,1:T(8,128)}, f32[128,4096]{0,1:T(8,128)}, f32[128,4096]{0,1:T(8,128)}, f32[128,4096]{0,1:T(8,128)}, f32[128,4096]{0,1:T(8,128)S(1)}) fusion(f32[128,4096]{0,1:T(8,128)} %get-tuple-element.1199, pred[]{:T(512)S(6)} %compare.18, f32[128,512]{0,1:T(8,128)S(1)} %get-tuple-element.1219, ...), kind=kLoop, calls=%fused_computation.50.clone.1 | loop fusion | flops 13631488 | bytes 22577668 | tf_op jit(solution)/shard_map/while/body/eval_jaxpr/add | solution.py:157
  229.3 9.5 %select_add_fusion.19 = (f32[128,4096]{0,1:T(8,128)}, f32[128,4096]{0,1:T(8,128)}, f32[128,4096]{0,1:T(8,128)}, f32[128,4096]{0,1:T(8,128)}, f32[128,4096]{0,1:T(8,128)S(1)}) fusion(f32[128,4096]{0,1:T(8,128)} %get-tuple-element.1199, pred[]{:T(512)S(6)} %compare.18, f32[128,512]{0,1:T(8,128)S(1)} %get-tuple-element.1219, ...), kind=kLoop, calls=%fused_computation.50.clone.1 | loop fusion | flops 13631488 | bytes 22577668 | tf_op jit(solution)/shard_map/while/body/eval_jaxpr/add | solution.py:157
  239.0 9.5 %select_add_fusion.19 = (f32[128,4096]{0,1:T(8,128)}, f32[128,4096]{0,1:T(8,128)}, f32[128,4096]{0,1:T(8,128)}, f32[128,4096]{0,1:T(8,128)}, f32[128,4096]{0,1:T(8,128)S(1)}) fusion(f32[128,4096]{0,1:T(8,128)} %get-tuple-element.1199, pred[]{:T(512)S(6)} %compare.18, f32[128,512]{0,1:T(8,128)S(1)} %get-tuple-element.1219, ...), kind=kLoop, calls=%fused_computation.50.clone.1 | loop fusion | flops 13631488 | bytes 22577668 | tf_op jit(solution)/shard_map/while/body/eval_jaxpr/add | solution.py:157
  248.8 9.5 %select_add_fusion.19 = (f32[128,4096]{0,1:T(8,128)}, f32[128,4096]{0,1:T(8,128)}, f32[128,4096]{0,1:T(8,128)}, f32[128,4096]{0,1:T(8,128)}, f32[128,4096]{0,1:T(8,128)S(1)}) fusion(f32[128,4096]{0,1:T(8,128)} %get-tuple-element.1199, pred[]{:T(512)S(6)} %compare.18, f32[128,512]{0,1:T(8,128)S(1)} %get-tuple-element.1219, ...), kind=kLoop, calls=%fused_computation.50.clone.1 | loop fusion | flops 13631488 | bytes 22577668 | tf_op jit(solution)/shard_map/while/body/eval_jaxpr/add | solution.py:157
  258.5 9.5 %select_add_fusion.19 = (f32[128,4096]{0,1:T(8,128)}, f32[128,4096]{0,1:T(8,128)}, f32[128,4096]{0,1:T(8,128)}, f32[128,4096]{0,1:T(8,128)}, f32[128,4096]{0,1:T(8,128)S(1)}) fusion(f32[128,4096]{0,1:T(8,128)} %get-tuple-element.1199, pred[]{:T(512)S(6)} %compare.18, f32[128,512]{0,1:T(8,128)S(1)} %get-tuple-element.1219, ...), kind=kLoop, calls=%fused_computation.50.clone.1 | loop fusion | flops 13631488 | bytes 22577668 | tf_op jit(solution)/shard_map/while/body/eval_jaxpr/add | solution.py:157
  275.0 9.3 %all_to_all.90 = f32[8,16,4,85]{3,2,1,0:T(4,128)S(1)} all-to-all(f32[8,16,4,85]{3,2,1,0:T(4,128)S(1)} %copy.325), channel_id=1, replica_groups=mesh['rows_0'=4,'rows_1'=4,'rows_2'=2,'fib'=4] {'rows_2','fib'}, dimensions={0} | all-to-all | bytes 348160 | tf_op jit(solution)/shard_map/all_to_all | solution.py:34
  284.4 9.2 %all_to_all.91 = f32[16,4,85]{2,1,0:T(4,128)S(1)} all-to-all(f32[16,4,85]{2,1,0:T(4,128)S(1)} %reduce_sum.201), channel_id=1, replica_groups=mesh['rows_0'=4,'rows_1'=4,'rows_2'=2,'fib'=4] {'rows_0','rows_1'}, dimensions={0} | all-to-all | bytes 43520 | tf_op jit(solution)/shard_map/all_to_all | solution.py:42
  296.3 8.1 %custom-call.39 = f32[4,22,22]{2,1,0:T(8,128)S(1)} custom-call(f32[4,22,22]{2,1,0:T(8,128)S(1)} %fusion.60), custom_call_target="Cholesky" | custom-call | tf_op jit(solution)/shard_map/jit(cholesky)/cholesky | solution.py:197
  304.6 6.8 %custom-call.41 = f32[4,1,22,22]{2,3,1,0:T(8,128)S(1)} custom-call(f32[4,1,22,22]{3,2,1,0:T(8,128)S(1)} %select_bitcast_fusion.1), custom_call_target="InvertDiagBlocksLowerTriangular" | custom-call | tf_op jit(solution)/shard_map/jit(_solve_triangular)/vmap()/triangular_solve | solution.py:199
  312.4 3.5 all-to-all-start.10
  316.0 6.3 %all-to-all-done.10 = f32[16,4,11]{2,1,0:T(4,128)S(1)} async-done(((f32[16,4,11]{2,1,0:T(4,128)}), f32[16,4,11]{2,1,0:T(4,128)S(1)}, u32[]{:S(2)}, u32[]{:S(2)}) %all-to-all-start.10) | async-done | bytes 2848 | tf_op jit(solution)/shard_map/all_to_all | solution.py:57
  322.9 3.5 all-to-all-start.8
  327.3 5.5 %all-to-all-done.8 = f32[16,4,11]{2,1,0:T(4,128)S(1)} async-done(((f32[16,4,11]{2,1,0:T(4,128)}), f32[16,4,11]{2,1,0:T(4,128)S(1)}, u32[]{:S(2)}, u32[]{:S(2)}) %all-to-all-start.8) | async-done | bytes 2848 | tf_op jit(solution)/shard_map/all_to_all | solution.py:57
  332.8 7.3 %all-to-all-start.11 = ((f32[8,1,704]{2,1,0:T(1,128)}), f32[8,1,704]{2,1,0:T(1,128)S(1)}, u32[]{:S(2)}, u32[]{:S(2)}) async-start(f32[8,1,704]{2,1,0:T(1,128)} %reshape.741), calls=%async_computation.11 | async-start | bytes 49152 | tf_op jit(solution)/shard_map/all_to_all | solution.py:57
  341.0 4.0 all-to-all-done.11
  345.0 3.6 all-to-all-start.9
  350.5 3.1 all-to-all-done.9
  355.1 47.4 %while.71 = (s32[]{:T(128)}, f32[128,4096]{0,1:T(8,128)S(1)}, f32[128,4096]{0,1:T(8,128)}, f32[128,4096]{0,1:T(8,128)}, f32[128,4096]{0,1:T(8,128)}, /*index=5*/...) while((s32[]{:T(128)}, f32[128,4096]{0,1:T(8,128)S(1)}, ...), condition=%wide.region_22.26_spmd.clone, body=%wide.region_21.25_spmd.clone.sunk | while | flops 13631491 | bytes 22660792 | solution.py:163
  355.4 8.1 %select_add_fusion.20 = (f32[128,4096]{0,1:T(8,128)}, f32[128,4096]{0,1:T(8,128)}, f32[128,4096]{0,1:T(8,128)}, f32[128,4096]{0,1:T(8,128)}, f32[128,4096]{0,1:T(8,128)S(1)}) fusion(f32[128,4096]{0,1:T(8,128)} %get-tuple-element.1241, pred[]{:T(512)S(6)} %compare.19, f32[128,512]{0,1:T(8,128)S(1)} %get-tuple-element.1261, ...), kind=kLoop, calls=%fused_computation.67.clone.1 | loop fusion | flops 13631488 | bytes 22577668 | tf_op jit(solution)/shard_map/while/body/eval_jaxpr/add | solution.py:157
  363.7 9.5 %select_add_fusion.20 = (f32[128,4096]{0,1:T(8,128)}, f32[128,4096]{0,1:T(8,128)}, f32[128,4096]{0,1:T(8,128)}, f32[128,4096]{0,1:T(8,128)}, f32[128,4096]{0,1:T(8,128)S(1)}) fusion(f32[128,4096]{0,1:T(8,128)} %get-tuple-element.1241, pred[]{:T(512)S(6)} %compare.19, f32[128,512]{0,1:T(8,128)S(1)} %get-tuple-element.1261, ...), kind=kLoop, calls=%fused_computation.67.clone.1 | loop fusion | flops 13631488 | bytes 22577668 | tf_op jit(solution)/shard_map/while/body/eval_jaxpr/add | solution.py:157
  373.5 9.5 %select_add_fusion.20 = (f32[128,4096]{0,1:T(8,128)}, f32[128,4096]{0,1:T(8,128)}, f32[128,4096]{0,1:T(8,128)}, f32[128,4096]{0,1:T(8,128)}, f32[128,4096]{0,1:T(8,128)S(1)}) fusion(f32[128,4096]{0,1:T(8,128)} %get-tuple-element.1241, pred[]{:T(512)S(6)} %compare.19, f32[128,512]{0,1:T(8,128)S(1)} %get-tuple-element.1261, ...), kind=kLoop, calls=%fused_computation.67.clone.1 | loop fusion | flops 13631488 | bytes 22577668 | tf_op jit(solution)/shard_map/while/body/eval_jaxpr/add | solution.py:157
  383.2 9.5 %select_add_fusion.20 = (f32[128,4096]{0,1:T(8,128)}, f32[128,4096]{0,1:T(8,128)}, f32[128,4096]{0,1:T(8,128)}, f32[128,4096]{0,1:T(8,128)}, f32[128,4096]{0,1:T(8,128)S(1)}) fusion(f32[128,4096]{0,1:T(8,128)} %get-tuple-element.1241, pred[]{:T(512)S(6)} %compare.19, f32[128,512]{0,1:T(8,128)S(1)} %get-tuple-element.1261, ...), kind=kLoop, calls=%fused_computation.67.clone.1 | loop fusion | flops 13631488 | bytes 22577668 | tf_op jit(solution)/shard_map/while/body/eval_jaxpr/add | solution.py:157
  393.0 9.5 %select_add_fusion.20 = (f32[128,4096]{0,1:T(8,128)}, f32[128,4096]{0,1:T(8,128)}, f32[128,4096]{0,1:T(8,128)}, f32[128,4096]{0,1:T(8,128)}, f32[128,4096]{0,1:T(8,128)S(1)}) fusion(f32[128,4096]{0,1:T(8,128)} %get-tuple-element.1241, pred[]{:T(512)S(6)} %compare.19, f32[128,512]{0,1:T(8,128)S(1)} %get-tuple-element.1261, ...), kind=kLoop, calls=%fused_computation.67.clone.1 | loop fusion | flops 13631488 | bytes 22577668 | tf_op jit(solution)/shard_map/while/body/eval_jaxpr/add | solution.py:157
  409.4 9.3 %all_to_all.92 = f32[8,16,4,85]{3,2,1,0:T(4,128)S(1)} all-to-all(f32[8,16,4,85]{3,2,1,0:T(4,128)S(1)} %copy.342), channel_id=1, replica_groups=mesh['rows_0'=4,'rows_1'=4,'rows_2'=2,'fib'=4] {'rows_2','fib'}, dimensions={0} | all-to-all | bytes 348160 | tf_op jit(solution)/shard_map/all_to_all | solution.py:34
  418.8 9.2 %all_to_all.93 = f32[16,4,85]{2,1,0:T(4,128)S(1)} all-to-all(f32[16,4,85]{2,1,0:T(4,128)S(1)} %reduce_sum.208), channel_id=1, replica_groups=mesh['rows_0'=4,'rows_1'=4,'rows_2'=2,'fib'=4] {'rows_0','rows_1'}, dimensions={0} | all-to-all | bytes 43520 | tf_op jit(solution)/shard_map/all_to_all | solution.py:42
  430.7 8.1 %custom-call.42 = f32[4,22,22]{2,1,0:T(8,128)S(1)} custom-call(f32[4,22,22]{2,1,0:T(8,128)S(1)} %fusion.56), custom_call_target="Cholesky" | custom-call | tf_op jit(solution)/shard_map/jit(cholesky)/cholesky | solution.py:197
  439.0 6.8 %custom-call.44 = f32[4,1,22,22]{2,3,1,0:T(8,128)S(1)} custom-call(f32[4,1,22,22]{3,2,1,0:T(8,128)S(1)} %select_bitcast_fusion), custom_call_target="InvertDiagBlocksLowerTriangular" | custom-call | tf_op jit(solution)/shard_map/jit(_solve_triangular)/vmap()/triangular_solve | solution.py:199
  446.9 3.5 all-to-all-start.16
  450.4 6.4 %all-to-all-done.16 = f32[16,4,11]{2,1,0:T(4,128)S(1)} async-done(((f32[16,4,11]{2,1,0:T(4,128)}), f32[16,4,11]{2,1,0:T(4,128)S(1)}, u32[]{:S(2)}, u32[]{:S(2)}) %all-to-all-start.16) | async-done | bytes 2848 | tf_op jit(solution)/shard_map/all_to_all | solution.py:57
  457.4 3.5 all-to-all-start.14
  461.8 5.5 %all-to-all-done.14 = f32[16,4,11]{2,1,0:T(4,128)S(1)} async-done(((f32[16,4,11]{2,1,0:T(4,128)}), f32[16,4,11]{2,1,0:T(4,128)S(1)}, u32[]{:S(2)}, u32[]{:S(2)}) %all-to-all-start.14) | async-done | bytes 2848 | tf_op jit(solution)/shard_map/all_to_all | solution.py:57
  467.2 7.3 %all-to-all-start.17 = ((f32[8,1,704]{2,1,0:T(1,128)}), f32[8,1,704]{2,1,0:T(1,128)S(1)}, u32[]{:S(2)}, u32[]{:S(2)}) async-start(f32[8,1,704]{2,1,0:T(1,128)} %reshape.745), calls=%async_computation.17 | async-start | bytes 49152 | tf_op jit(solution)/shard_map/all_to_all | solution.py:57
  475.5 4.0 all-to-all-done.17
  479.5 3.6 all-to-all-start.15
  484.9 3.1 all-to-all-done.15
  489.6 24.0 %while.68 = (s32[]{:T(128)}, bf16[5,128,4096]{2,1,0:T(8,128)(2,1)}, bf16[5,128,4096]{1,2,0:T(8,128)(2,1)}, f32[5,128]{1,0:T(8,128)S(1)}, f32[5,4096]{1,0:T(8,128...) while((s32[]{:T(128)}, bf16[5,128,4096]{2,1,0:T(8,128)(2,1)}, ...), condition=%wide.region_31.35_spmd.clone, body=%wide.region_30.34_spmd.clone.sunk | while | flops 4718594 | bytes 6932617 | solution.py:210
  489.8 3.0 fusion.169
  494.6 3.0 fusion.169
  499.4 3.0 fusion.169
  504.2 3.0 fusion.169
  509.0 3.0 fusion.169
  (342 shorter events, 73.7 us)
Async XLA Ops:
  0.6 64.6 %copy-start = (f32[20]{0:T(128)S(1)}, f32[20]{0:T(128)}, u32[]{:S(2)}) copy-start(f32[20]{0:T(128)} %param.24) | copy-start | bytes 244
  68.8 7.8 %copy-start.11 = (f32[5,512]{1,0:T(8,128)S(1)}, f32[5,512]{1,0:T(8,128)}, u32[]{:S(2)}) copy-start(f32[5,512]{1,0:T(8,128)} %param.22) | copy-start | bytes 30724
  127.5 2.3 copy-start.8
  130.4 3.2 copy-start.9
  134.5 24.7 %copy-start.10 = (f32[21,121]{1,0:T(8,128)S(1)}, f32[21,121]{1,0:T(8,128)}, u32[]{:S(2)}) copy-start(f32[21,121]{1,0:T(8,128)} %constant.258.clone) | copy-start | bytes 30496
  135.0 42.3 %copy-start.12 = (f32[4,11]{1,0:T(4,128)S(1)}, f32[4,11]{1,0:T(4,128)}, u32[]{:S(2)}) copy-start(f32[4,11]{1,0:T(4,128)} %param.27) | copy-start | bytes 532
  135.0 42.2 %copy-start.13 = (f32[4,11]{1,0:T(4,128)S(1)}, f32[4,11]{1,0:T(4,128)}, u32[]{:S(2)}) copy-start(f32[4,11]{1,0:T(4,128)} %param.26) | copy-start | bytes 532
  136.8 10.6 %all-to-all-start = ((f32[8,16,4,85]{3,2,1,0:T(4,128)}), f32[8,16,4,85]{3,2,1,0:T(4,128)S(1)}, u32[]{:S(2)}, u32[]{:S(2)}) async-start(f32[8,16,4,85]{3,2,1,0:T(4,128)} %copy.308), calls=%async_computation | async-start | bytes 524288 | tf_op jit(solution)/shard_map/all_to_all | solution.py:34
  148.1 11.1 %all-to-all-start.1 = ((f32[16,4,85]{2,1,0:T(4,128)}), f32[16,4,85]{2,1,0:T(4,128)S(1)}, u32[]{:S(2)}, u32[]{:S(2)}) async-start(f32[16,4,85]{2,1,0:T(4,128)} %reduce_sum.194), calls=%async_computation.1 | async-start | bytes 65536 | tf_op jit(solution)/shard_map/all_to_all | solution.py:42
  178.0 9.9 %all-to-all-start.4 = ((f32[16,4,11]{2,1,0:T(4,128)}), f32[16,4,11]{2,1,0:T(4,128)S(1)}, u32[]{:S(2)}, u32[]{:S(2)}) async-start(f32[16,4,11]{2,1,0:T(4,128)} %broadcast_in_dim.74), calls=%async_computation.4 | async-start | bytes 65536 | tf_op jit(solution)/shard_map/all_to_all | solution.py:57
  188.5 9.9 %all-to-all-start.2 = ((f32[16,4,11]{2,1,0:T(4,128)}), f32[16,4,11]{2,1,0:T(4,128)S(1)}, u32[]{:S(2)}, u32[]{:S(2)}) async-start(f32[16,4,11]{2,1,0:T(4,128)} %broadcast_in_dim.71), calls=%async_computation.2 | async-start | bytes 65536 | tf_op jit(solution)/shard_map/all_to_all | solution.py:57
  198.3 12.2 %all-to-all-start.5 = ((f32[8,1,704]{2,1,0:T(1,128)}), f32[8,1,704]{2,1,0:T(1,128)S(1)}, u32[]{:S(2)}, u32[]{:S(2)}) async-start(f32[8,1,704]{2,1,0:T(1,128)} %reshape.737), calls=%async_computation.5 | async-start | bytes 49152 | tf_op jit(solution)/shard_map/all_to_all | solution.py:57
  210.5 8.5 %all-to-all-start.3 = ((f32[8,1,704]{2,1,0:T(1,128)}), f32[8,1,704]{2,1,0:T(1,128)S(1)}, u32[]{:S(2)}, u32[]{:S(2)}) async-start(f32[8,1,704]{2,1,0:T(1,128)} %reshape.735), calls=%async_computation.3 | async-start | bytes 49152 | tf_op jit(solution)/shard_map/all_to_all | solution.py:57
  268.1 2.7 copy-start.2
  268.1 3.6 copy-start.3
  270.7 1.8 copy-start.4
  312.4 9.9 %all-to-all-start.10 = ((f32[16,4,11]{2,1,0:T(4,128)}), f32[16,4,11]{2,1,0:T(4,128)S(1)}, u32[]{:S(2)}, u32[]{:S(2)}) async-start(f32[16,4,11]{2,1,0:T(4,128)} %broadcast_in_dim.83), calls=%async_computation.10 | async-start | bytes 65536 | tf_op jit(solution)/shard_map/all_to_all | solution.py:57
  322.9 9.9 %all-to-all-start.8 = ((f32[16,4,11]{2,1,0:T(4,128)}), f32[16,4,11]{2,1,0:T(4,128)S(1)}, u32[]{:S(2)}, u32[]{:S(2)}) async-start(f32[16,4,11]{2,1,0:T(4,128)} %broadcast_in_dim.80), calls=%async_computation.8 | async-start | bytes 65536 | tf_op jit(solution)/shard_map/all_to_all | solution.py:57
  332.8 12.2 %all-to-all-start.11 = ((f32[8,1,704]{2,1,0:T(1,128)}), f32[8,1,704]{2,1,0:T(1,128)S(1)}, u32[]{:S(2)}, u32[]{:S(2)}) async-start(f32[8,1,704]{2,1,0:T(1,128)} %reshape.741), calls=%async_computation.11 | async-start | bytes 49152 | tf_op jit(solution)/shard_map/all_to_all | solution.py:57
  345.0 8.5 %all-to-all-start.9 = ((f32[8,1,704]{2,1,0:T(1,128)}), f32[8,1,704]{2,1,0:T(1,128)S(1)}, u32[]{:S(2)}, u32[]{:S(2)}) async-start(f32[8,1,704]{2,1,0:T(1,128)} %reshape.739), calls=%async_computation.9 | async-start | bytes 49152 | tf_op jit(solution)/shard_map/all_to_all | solution.py:57
  402.5 2.7 copy-start.5
  402.5 3.6 copy-start.6
  405.2 1.8 copy-start.7
  446.3 43.0 %copy-start.14 = (f32[4,11]{1,0:T(4,128)}, f32[4,11]{1,0:T(4,128)S(1)}, u32[]{:S(2)}) copy-start(f32[4,11]{1,0:T(4,128)S(1)} %get-tuple-element.814) | copy-start | bytes 532
  446.3 43.0 %copy-start.15 = (f32[4,11]{1,0:T(4,128)}, f32[4,11]{1,0:T(4,128)S(1)}, u32[]{:S(2)}) copy-start(f32[4,11]{1,0:T(4,128)S(1)} %get-tuple-element.815) | copy-start | bytes 532
  446.9 9.9 %all-to-all-start.16 = ((f32[16,4,11]{2,1,0:T(4,128)}), f32[16,4,11]{2,1,0:T(4,128)S(1)}, u32[]{:S(2)}, u32[]{:S(2)}) async-start(f32[16,4,11]{2,1,0:T(4,128)} %broadcast_in_dim.91), calls=%async_computation.16 | async-start | bytes 65536 | tf_op jit(solution)/shard_map/all_to_all | solution.py:57
  457.4 9.9 %all-to-all-start.14 = ((f32[16,4,11]{2,1,0:T(4,128)}), f32[16,4,11]{2,1,0:T(4,128)S(1)}, u32[]{:S(2)}, u32[]{:S(2)}) async-start(f32[16,4,11]{2,1,0:T(4,128)} %broadcast_in_dim.88), calls=%async_computation.14 | async-start | bytes 65536 | tf_op jit(solution)/shard_map/all_to_all | solution.py:57
  467.2 12.2 %all-to-all-start.17 = ((f32[8,1,704]{2,1,0:T(1,128)}), f32[8,1,704]{2,1,0:T(1,128)S(1)}, u32[]{:S(2)}, u32[]{:S(2)}) async-start(f32[8,1,704]{2,1,0:T(1,128)} %reshape.745), calls=%async_computation.17 | async-start | bytes 49152 | tf_op jit(solution)/shard_map/all_to_all | solution.py:57
  479.5 8.5 %all-to-all-start.15 = ((f32[8,1,704]{2,1,0:T(1,128)}), f32[8,1,704]{2,1,0:T(1,128)S(1)}, u32[]{:S(2)}, u32[]{:S(2)}) async-start(f32[8,1,704]{2,1,0:T(1,128)} %reshape.743), calls=%async_computation.15 | async-start | bytes 49152 | tf_op jit(solution)/shard_map/all_to_all | solution.py:57
  513.6 0.7 copy-start.1
where the time goes:
time: 517 us; the launch traced here: 514 us
  other arithmetic  222 us (43%)
  blocking collectives  100 us (19%)
  waiting for transfers between devices  69.2 us (13%)
  starting transfers between devices  62.4 us (12%)
  local copies, waits for them, and re-layouts  45.8 us (9%)
  matrix products  12 us (2%)
    add x15, other arithmetic, accumulate_one_lamp(): carry[4] + resid * widen  139 us
    all_gather x1, blocking collectives, sent_together(): lax.all_gather(both, axis, axis=dim, tiled=True)  63.3 us
    all_to_all x12, waiting for transfers between devices, from_everyone(): lax.all_to_all(jnp.broadcast_to(x[None], (peers, *x.shape)), axis, 0, 0,...  56.2 us
    all_to_all x12, starting transfers between devices, from_everyone(): lax.all_to_all(jnp.broadcast_to(x[None], (peers, *x.shape)), axis, 0, 0,...  53.7 us
    another operation x10, other arithmetic, solve_step(): factor = jnp.linalg.cholesky(matrix)  24.7 us
    another operation x7, other arithmetic, solve_step(): jax.scipy.linalg.solve_triangular(factor, inner, lower=True, trans=1)  20.6 us
    all_to_all x2, blocking collectives, sum_at_owner(): lax.all_to_all(blocks, axis, split_axis=0, concat_axis=0, tiled=True)  18.7 us
    all_to_all x2, blocking collectives, sum_in_two_steps(): lax.all_to_all(nearer, far, split_axis=0, concat_axis=0, tiled=True)  18.5 us
  transfers between devices with their start and end apart: 14, of which 14 were waited for; matrix products, arithmetic and copies ran while one was open for 2% of the time, Pallas kernels for 0%

commit v1 on v0

v1 whole, which is shorter than its diff:
```python
import functools
import math

import jax
import jax.numpy as jnp
import numpy as np
from jax import lax
from jax.experimental import pallas as pl
from jax.experimental.pallas import tpu as pltpu
from jax.sharding import PartitionSpec as P

K = 11
PIX = 8
WIN = 8
ITERS = 3
LANES = 128
NDEV = 128
PLANES = 4
PER = 32
MINE = 4
SLOT = 32
KAPPA = math.sqrt(0.5 / math.log(2.0))
F32 = jnp.float32
BF16 = jnp.bfloat16
MESH = pl.DeviceIdType.MESH
HIGH = lax.Precision.HIGHEST


def adams_factor(order):
    value = 1.0
    for index in range(1, order + 1):
        value = value * (2.0 * index - 1.0) / index
    return value


def product_table():
    table = np.zeros((2 * K - 1, K, K))
    for a in range(K):
        for b in range(K):
            for m in range(min(a, b) + 1):
                target = a + b - 2 * m
                weight = adams_factor(m) * adams_factor(a - m) * adams_factor(b - m)
                weight = weight / adams_factor(a + b - m)
                weight = weight * (2.0 * target + 1.0) / (2.0 * (a + b - m) + 1.0)
                table[target, a, b] += weight
    return table


MOMENTS = 2 * K - 1
GRAD0 = 3 * MOMENTS


def link_table():
    link = product_table()
    out = np.zeros((LANES, 24 * SLOT))
    for i in range(2 * K):
        for k in range(2 * K):
            which = (i >= K) + (k >= K)
            damp = 1.5 if i == k else 1.0
            out[which * MOMENTS : (which + 1) * MOMENTS, i * SLOT + k] = damp * link[:, i % K, k % K]
        out[GRAD0 + i, i * SLOT + 2 * K] = 1.0
    high = jnp.asarray(out, F32).astype(BF16)
    low = (jnp.asarray(out, F32) - high.astype(F32)).astype(BF16)
    return jnp.concatenate([high, low], axis=0)


def iota(shape, dim):
    return lax.broadcasted_iota(jnp.int32, shape, dim)


def legendre(t, count):
    polys = [jnp.ones_like(t), t]
    for n in range(1, count - 1):
        polys.append(((2 * n + 1) * t * polys[n] - n * polys[n - 1]) / (n + 1))
    return polys[:count]


def t_of(row, total):
    return (2.0 * row.astype(F32) + 1.0) / total - 1.0


def split(x):
    high = x.astype(BF16)
    return high, (x - high.astype(F32)).astype(BF16)


def lit_row(starts, lamp, lines, first):
    row = first + iota((1, LANES), 1)
    hit = jnp.zeros((1, LANES), F32)
    for i in range(lines):
        low = starts[lamp, i]
        hit = jnp.where((row >= low) & (row < low + WIN), 1.0, hit)
    return hit


def base_row(fiber_bundle, bundle_width, bundles):
    out = jnp.zeros(fiber_bundle.shape, F32)
    for b in range(bundles):
        out = jnp.where(fiber_bundle == b, bundle_width[b], out)
    return out


def fit_kernel(
    lamps, lines, bundles, nrow,
    starts, bundle_width, fiber_bundle, amplitude, trace, width, link_hbm, frames_hbm,
    out,
    frames, ft, fq, a2, invb, mix, litc, px, tb, xq, whi, wlo, link, row, ag, mom, rs,
    in_sem, link_sem, ag_send, ag_recv, rs_send, rs_recv,
):
    my_row, my_fib = lax.axis_index("rows"), lax.axis_index("fib")
    me = my_row * 4 + my_fib
    my_z, my_in = me // PER, me % PER
    first = my_row * LANES

    for lamp in range(lamps):
        pltpu.make_async_copy(frames_hbm.at[lamp], frames.at[lamp], in_sem.at[lamp]).start()
    pltpu.make_async_copy(link_hbm, link, link_sem).start()

    barrier = pltpu.get_barrier_semaphore()

    @pl.loop(1, NDEV)
    def _(i):
        peer = (me + i) % NDEV
        pl.semaphore_signal(barrier, inc=1, device_id=(peer // 4, peer % 4), device_id_type=MESH)

    def tell_everyone(step):
        pltpu.make_async_copy(row.at[step], ag.at[step, me], ag_recv.at[step, my_z]).start()

        @pl.loop(1, NDEV)
        def _(i):
            peer = (me + i) % NDEV
            pltpu.make_async_remote_copy(
                src_ref=row.at[step],
                dst_ref=ag.at[step, me],
                send_sem=ag_send.at[step],
                recv_sem=ag_recv.at[step, my_z],
                device_id=(peer // 4, peer % 4),
                device_id_type=MESH,
            ).start()

    row[0] = jnp.zeros((1, LANES), F32)
    for j in range(MINE):
        row[0, :, SLOT * j : SLOT * j + K] = trace[j : j + 1, :]
        row[0, :, SLOT * j + K : SLOT * j + 2 * K] = width[j : j + 1, :]

    px[...] = jnp.zeros(px.shape, BF16)
    sub = iota((SLOT, LANES), 0)
    polys = legendre(t_of(first + iota((1, LANES), 1), nrow), K)
    for part in range(2):
        table = jnp.zeros((SLOT, LANES), F32)
        for k in range(K):
            table = jnp.where(sub == k + part * K, (1.0, -1.0)[part] * polys[k], table)
        high, low = split(table)
        for j in range(MINE):
            lanes = pl.ds((2 * j + part) * LANES, LANES)
            px[pl.ds(SLOT * j, SLOT), lanes] = high
            px[pl.ds(LANES + SLOT * j, SLOT), lanes] = low

    @pl.loop(0, LANES // 16)
    def _(b):
        lane = iota((16, LANES), 1)
        degree = jnp.where(lane < GRAD0, lane % MOMENTS, (lane - GRAD0) % K)
        degree = jnp.where(lane < GRAD0 + 2 * K, degree, -1)
        wide = legendre(t_of(first + b * 16 + iota((16, LANES), 0), nrow), MOMENTS)
        table = jnp.zeros((16, LANES), F32)
        for k in range(MOMENTS):
            table = jnp.where(degree == k, wide[k], table)
        table = table * jnp.where(lane < GRAD0, KAPPA**-4, KAPPA**-2)
        ends = [0, MOMENTS, 2 * MOMENTS, GRAD0, GRAD0 + K, GRAD0 + 2 * K]
        for a in range(5):
            inside = (lane >= ends[a]) & (lane < ends[a + 1])
            high, low = split(jnp.where(inside, table, 0.0))
            rows = pl.ds(pl.multiple_of(a * LANES + b * 16, 16), 16)
            tb[rows, 0:LANES] = high
            tb[rows, LANES : 2 * LANES] = low

    pl.semaphore_wait(barrier, NDEV - 1)
    tell_everyone(0)

    lits = [lit_row(starts, lamp, lines, first) for lamp in range(lamps)]
    for lamp in range(lamps):
        litc[lamp] = jnp.transpose(jnp.broadcast_to(lits[lamp], (LANES, LANES)))
    base = base_row(fiber_bundle[...], bundle_width, bundles)
    sub8 = iota((8, LANES), 0)
    sub8w = iota((8, amplitude.shape[1]), 0)
    amp = jnp.zeros(sub8w.shape, F32)
    lit8 = jnp.zeros((8, LANES), F32)
    for lamp in range(lamps):
        amp = jnp.where(sub8w == lamp, amplitude[lamp : lamp + 1, :], amp)
        lit8 = jnp.where(sub8 == lamp, lits[lamp], lit8)
    left = jnp.where(sub8w == lamps, KAPPA / base, amp * amp)
    right = jnp.concatenate([lit8, jnp.where(sub8 == lamps, 1.0, jnp.zeros((8, LANES), F32))], axis=1)
    mixed = lax.dot_general(
        jnp.transpose(left), right, (((1,), (0,)), ((), ())), precision=HIGH, preferred_element_type=F32
    )
    for part, dest in enumerate((a2, invb)):
        mix[...] = mixed[:, part * LANES : (part + 1) * LANES]
        for j in range(MINE):
            dest[j] = mix[pl.ds(j, NDEV, stride=MINE), :]

    for lamp in range(lamps):
        pltpu.make_async_copy(frames_hbm.at[lamp], frames.at[lamp], in_sem.at[lamp]).wait()
    spread = iota((8, LANES), 1) // PIX
    for b in range(32):
        cols = pl.ds(b * LANES, LANES)
        part = lax.slice_in_dim(amp, (b // 8) * LANES, (b // 8 + 1) * LANES, axis=1)
        bright = jnp.take_along_axis(part, spread + 16 * (b % 8), axis=1)
        total = jnp.zeros((LANES, LANES), F32)
        for lamp in range(lamps):
            weight = litc[lamp] * bright[lamp : lamp + 1, :]
            total = total + weight * frames[lamp, :, cols].astype(F32)
        ft[pl.ds(b * LANES, LANES), :] = jnp.transpose(total)

    @pl.loop(0, 32)
    def _(q):
        fq[q] = ft[pl.ds(q, NDEV, stride=32), :]

    pltpu.make_async_copy(link_hbm, link, link_sem).wait()

    def one_plane(step, hop):
        z = (my_z + hop) % PLANES
        d0 = pl.multiple_of(z * PER, PER)
        here = ag.at[step, pl.ds(d0, PER)]
        pltpu.make_async_copy(here, here, ag_recv.at[step, z]).wait()
        coef = ag[step, pl.ds(d0, PER), 0, :]
        high, low = split(coef)
        lhs = jnp.concatenate(
            [jnp.concatenate([high, high], axis=1), jnp.concatenate([low, low], axis=1)], axis=0
        )
        both = jnp.dot(lhs, px[...], preferred_element_type=F32)
        xq[...] = both[0:PER] + both[PER : 2 * PER]

        for j in range(MINE):
            for half in range(2):
                rows = pl.ds(half * 16, 16)
                drows = pl.ds(pl.multiple_of(d0 + half * 16, 16), 16)
                x = xq[rows, (2 * j) * LANES : (2 * j + 1) * LANES]
                inv = jnp.exp(xq[rows, (2 * j + 1) * LANES : (2 * j + 2) * LANES]) * invb[j, drows, :]
                bright2 = a2[j, drows, :]
                sxx = sxs = sss = hx = hs = jnp.zeros((16, LANES), F32)
                for p in range(PIX):
                    u = ((p - (PIX - 1) / 2.0) - x) * inv
                    g = jnp.exp2(-(u * u))
                    gu = g * u
                    m = gu * gu
                    n = m * u
                    tg = (fq[PIX * j + p, drows, :] - bright2 * g) * gu
                    sxx = sxx + m
                    sxs = sxs + n
                    sss = sss + n * u
                    hx = hx + tg
                    hs = hs + tg * u
                binv = bright2 * inv
                sums = (binv * inv * sxx, binv * sxs, bright2 * sss, inv * hx, hs)
                wrows = pl.ds(j * PER + half * 16, 16)
                for a in range(5):
                    h, l = split(sums[a])
                    whi[wrows, a * LANES : (a + 1) * LANES] = h
                    wlo[wrows, a * LANES : (a + 1) * LANES] = l
        one = jnp.dot(whi[...], tb[...], preferred_element_type=F32)
        two = jnp.dot(wlo[...], tb[:, 0:LANES], preferred_element_type=F32)
        moments = one[:, 0:LANES] + one[:, LANES : 2 * LANES] + two
        for j in range(MINE):
            mom[step, pl.ds(d0, PER), j, :] = moments[j * PER : (j + 1) * PER, :]

        @pl.loop(1 if hop == 0 else 0, PER)
        def _(i):
            peer = d0 + (my_in + i) % PER
            pltpu.make_async_remote_copy(
                src_ref=mom.at[step, peer],
                dst_ref=rs.at[step, me],
                send_sem=rs_send.at[step],
                recv_sem=rs_recv.at[step],
                device_id=(peer // 4, peer % 4),
                device_id_type=MESH,
            ).start()

        if hop == 0:
            pltpu.make_async_copy(mom.at[step, me], rs.at[step, me], rs_recv.at[step]).start()

    def solve(step):
        pltpu.make_async_copy(rs.at[step], rs.at[step], rs_recv.at[step]).wait()
        parts = [rs[step, pl.ds(32 * i, 32)].sum(axis=0) for i in range(4)]
        total = (parts[0] + parts[1]) + (parts[2] + parts[3])
        high = total.astype(BF16).astype(F32)
        both = jnp.concatenate([high, total - high], axis=0)
        lhs = jnp.concatenate([both, both], axis=1).astype(BF16)
        both = jnp.dot(lhs, link[...], preferred_element_type=F32)
        both = both[0:MINE] + both[MINE : 2 * MINE]
        lane = iota((MINE, LANES), 1)
        system = []
        for i in range(2 * K):
            block = both[:, (i // 4) * LANES : (i // 4 + 1) * LANES]
            if i % 4:
                block = pltpu.roll(block, LANES - SLOT * (i % 4), axis=1)
            system.append(jnp.where(lane == i, block + 1.0, block))
        for k in range(2 * K):
            scaled = system[k] * (1.0 / system[k][:, k : k + 1])
            for i in range(2 * K):
                if i != k:
                    system[i] = system[i] - system[i][:, k : k + 1] * scaled
            system[k] = scaled
        found = jnp.zeros((MINE, LANES), F32)
        for i in range(2 * K):
            found = jnp.where(lane % SLOT == i, system[i][:, 2 * K : 2 * K + 1], found)
        found = jnp.where(iota((MINE, LANES), 0) == lane // SLOT, found, 0.0)
        row[step + 1] = row[step] + found.sum(axis=0, keepdims=True)

    @pl.loop(0, ITERS)
    def _(step):
        for hop in (0, 1, 3, 2):
            one_plane(step, hop)
        solve(step)
        tell_everyone(step + 1)
        sent = mom.at[step, pl.ds(0, NDEV - 1)]
        pltpu.make_async_copy(sent, sent, rs_send.at[step]).wait()
        told = ag.at[step, pl.ds(0, NDEV - 1)]
        pltpu.make_async_copy(told, told, ag_send.at[step]).wait()

    for z in range(PLANES):
        here = ag.at[ITERS, pl.ds(z * PER, PER)]
        pltpu.make_async_copy(here, here, ag_recv.at[ITERS, z]).wait()
    out[...] = ag[ITERS, :, 0, :]
    told = ag.at[ITERS, pl.ds(0, NDEV - 1)]
    pltpu.make_async_copy(told, told, ag_send.at[ITERS]).wait()


def fit(starts, bundle_width, fiber_bundle, amplitude, trace, width, frames, nrow):
    lamps, rows, cols = frames.shape
    vmem = pl.BlockSpec(memory_space=pltpu.VMEM)
    smem = pl.BlockSpec(memory_space=pltpu.SMEM)
    hbm = pl.BlockSpec(memory_space=pl.ANY)
    dma = pltpu.SemaphoreType.DMA
    kernel = functools.partial(fit_kernel, lamps, starts.shape[1], bundle_width.shape[0], nrow)
    return pl.pallas_call(
        kernel,
        out_shape=jax.ShapeDtypeStruct((NDEV, LANES), F32),
        in_specs=[smem, smem, vmem, vmem, vmem, vmem, hbm, hbm],
        out_specs=vmem,
        scratch_shapes=[
            pltpu.VMEM((lamps, rows, cols), BF16),
            pltpu.VMEM((cols, LANES), F32),
            pltpu.VMEM((32, NDEV, LANES), F32),
            pltpu.VMEM((MINE, NDEV, LANES), F32),
            pltpu.VMEM((MINE, NDEV, LANES), F32),
            pltpu.VMEM((MINE * NDEV, LANES), F32),
            pltpu.VMEM((lamps, LANES, LANES), F32),
            pltpu.VMEM((2 * LANES, 8 * LANES), BF16),
            pltpu.VMEM((5 * LANES, 2 * LANES), BF16),
            pltpu.VMEM((PER, 8 * LANES), F32),
            pltpu.VMEM((LANES, 5 * LANES), BF16),
            pltpu.VMEM((LANES, 5 * LANES), BF16),
            pltpu.VMEM((2 * LANES, 24 * SLOT), BF16),
            pltpu.VMEM((ITERS + 1, 1, LANES), F32),
            pltpu.VMEM((ITERS + 1, NDEV, 1, LANES), F32),
            pltpu.VMEM((ITERS, NDEV, MINE, LANES), F32),
            pltpu.VMEM((ITERS, NDEV, MINE, LANES), F32),
            dma((lamps,)),
            dma,
            dma((ITERS + 1,)),
            dma((ITERS + 1, PLANES)),
            dma((ITERS,)),
            dma((ITERS,)),
        ],
        compiler_params=pltpu.CompilerParams(
            collective_id=0, has_side_effects=True, vmem_limit_bytes=40 << 20
        ),
        name="fit",
    )(starts, bundle_width, fiber_bundle, amplitude, trace, width, link_table(), frames)


def residual_kernel(
    lamps, lines, bundles, nrow,
    starts, bundle_width, fiber_bundle, amplitude, coef, frames,
    trace_out, width_out, out,
    table, rates, litc, ptab,
):
    my_row = lax.axis_index("rows")
    me = my_row * 4 + lax.axis_index("fib")
    first = my_row * LANES
    step = pl.program_id(0)
    wide = frames.shape[2]

    @pl.when(step == 0)
    def _():
        mine = coef[pl.ds(me, 1), :]
        for j in range(MINE):
            trace_out[j : j + 1, :] = mine[:, SLOT * j : SLOT * j + K]
            width_out[j : j + 1, :] = mine[:, SLOT * j + K : SLOT * j + 2 * K]
        for lamp in range(lamps):
            litc[lamp] = jnp.transpose(
                jnp.broadcast_to(lit_row(starts, lamp, lines, first), (LANES, LANES))
            )
        lane = iota((LANES, LANES), 1)
        polys = legendre(t_of(first + iota((LANES, LANES), 0), nrow), K)
        for part in range(2):
            tab = jnp.zeros((LANES, LANES), F32)
            for k in range(K):
                tab = jnp.where(lane % SLOT == k + part * K, (1.0, -1.0)[part] * polys[k], tab)
            high = tab.astype(BF16).astype(F32)
            tab = jnp.where(lane < 2 * SLOT, high, jnp.where(lane < 3 * SLOT, tab - high, 0.0))
            ptab[pl.ds(part * LANES, LANES), :] = tab.astype(BF16)
        base = base_row(fiber_bundle[...], bundle_width, bundles)
        fibers = fiber_bundle.shape[1]
        sub8w = iota((8, fibers), 0)
        rate = jnp.broadcast_to(KAPPA / base, (8, fibers))
        for lamp in range(lamps):
            rate = jnp.where(sub8w == lamp, amplitude[lamp : lamp + 1, :], rate)
        turned = jnp.transpose(coef[...])
        lane = iota((SLOT, LANES), 1)
        lane8 = iota((8, LANES), 1) // PIX
        for fb in range(4):
            pick = 32 * fb + lane // MINE
            named = jnp.zeros((SLOT, LANES), F32)
            for j in range(MINE):
                got = jnp.take_along_axis(turned[SLOT * j : SLOT * (j + 1), :], pick, axis=1)
                named = jnp.where(lane % MINE == j, got, named)
            part = rate[:, fb * LANES : (fb + 1) * LANES]
            for b in range(8):
                cols = pl.ds((8 * fb + b) * LANES, LANES)
                got = jnp.take_along_axis(named, lane // PIX + 16 * b, axis=1)
                high, low = split(got)
                table[0:SLOT, cols] = high
                table[SLOT : 2 * SLOT, cols] = low
                table[2 * SLOT : 3 * SLOT, cols] = high
                table[3 * SLOT : 4 * SLOT, cols] = jnp.zeros((SLOT, LANES), BF16)
                rates[:, cols] = jnp.take_along_axis(part, lane8 + 16 * b, axis=1)

    offset = (iota((1, LANES), 1) % PIX).astype(F32) - (PIX - 1) / 2.0
    here = pl.ds(pl.multiple_of(step * wide, LANES), wide)
    xq = jnp.dot(ptab[...], table[:, here], preferred_element_type=F32)
    rate = rates[:, here]
    for b in range(wide // LANES):
        cols = slice(b * LANES, (b + 1) * LANES)
        x, q = xq[0:LANES, cols], xq[LANES : 2 * LANES, cols]
        u = (offset - x) * (jnp.exp(q) * rate[lamps : lamps + 1, cols])
        g = jnp.exp2(-(u * u))
        for lamp in range(lamps):
            model = (litc[lamp] * rate[lamp : lamp + 1, cols]) * g
            out[lamp, :, cols] = (frames[lamp, :, cols].astype(F32) - model).astype(BF16)


def residual(starts, bundle_width, fiber_bundle, amplitude, coef, frames, nrow):
    lamps, rows, cols = frames.shape
    wide = 512
    vmem = pl.BlockSpec(memory_space=pltpu.VMEM)
    smem = pl.BlockSpec(memory_space=pltpu.SMEM)
    strip = pl.BlockSpec((lamps, rows, wide), lambda i: (0, 0, i))
    kernel = functools.partial(residual_kernel, lamps, starts.shape[1], bundle_width.shape[0], nrow)
    small = jax.ShapeDtypeStruct((MINE, K), F32)
    return pl.pallas_call(
        kernel,
        grid=(cols // wide,),
        out_shape=(small, small, jax.ShapeDtypeStruct(frames.shape, BF16)),
        in_specs=[smem, smem, vmem, vmem, vmem, strip],
        out_specs=(vmem, vmem, strip),
        scratch_shapes=[
            pltpu.VMEM((LANES, cols), BF16),
            pltpu.VMEM((8, cols), F32),
            pltpu.VMEM((lamps, LANES, LANES), F32),
            pltpu.VMEM((2 * LANES, LANES), BF16),
        ],
        compiler_params=pltpu.CompilerParams(vmem_limit_bytes=30 << 20),
        name="residual",
    )(starts, bundle_width, fiber_bundle, amplitude, coef, frames)


def body(frames, amplitude, line_start, bundle_width, fiber_bundle, trace_coef, width_coef):
    nrow = frames.shape[1] * lax.axis_size("rows")
    bundle = fiber_bundle.reshape(1, -1)
    coef = fit(line_start, bundle_width, bundle, amplitude, trace_coef, width_coef, frames, nrow)
    return residual(line_start, bundle_width, bundle, amplitude, coef, frames, nrow)


def solution(mesh):
    placed = (
        P("fib", "rows", None),
        P("fib", None),
        P("fib", None),
        P(),
        P(),
        P(("rows", "fib"), None),
        P(("rows", "fib"), None),
    )
    return jax.shard_map(
        body,
        mesh=mesh,
        in_specs=placed,
        out_specs=(P(("rows", "fib"), None), P(("rows", "fib"), None), P("fib", "rows", None)),
        check_vma=False,
    )
```

time: 517 us -> 97.3 us (0.19)
  other arithmetic: 222 us -> 0 us
  blocking collectives: 100 us -> 0 us
  Pallas kernels: 0 us -> 88.7 us
  waiting for transfers between devices: 69.2 us -> 0 us
  starting transfers between devices: 62.4 us -> 0 us
  local copies, waits for them, and re-layouts: 45.8 us -> 7.58 us
  matrix products: 12 us -> 0 us
    add x26 -> x0, other arithmetic: 140 us -> none  [the longest x15 139 us: accumulate_one_lamp(): carry[4] + resid * widen]
    pallas_call x0 -> x2, Pallas kernels: none -> 88.7 us  [the longest x1 80.8 us: fit(): pl.pallas_call(kernel, out_shape=jax.ShapeDtypeStruct((NDEV, LANES), F32)...]
    all_to_all x14 -> x0, waiting for transfers between devices: 69.2 us -> none  [the longest x12 56.2 us: from_everyone(): lax.all_to_all(jnp.broadcast_to(x[None], (peers, *x.shape)), axis, 0, 0,...]
    all_gather x1 -> x0, blocking collectives: 63.3 us -> none  [sent_together(): lax.all_gather(both, axis, axis=dim, tiled=True)]
    all_to_all x14 -> x0, starting transfers between devices: 62.4 us -> none  [the longest x12 53.7 us: from_everyone(): lax.all_to_all(jnp.broadcast_to(x[None], (peers, *x.shape)), axis, 0, 0,...]
    another operation x17 -> x0, other arithmetic: 45.3 us -> none  [the longest x10 24.7 us: solve_step(): factor = jnp.linalg.cholesky(matrix)]
    all_to_all x4 -> x0, blocking collectives: 37.2 us -> none  [the longest x2 18.7 us: sum_at_owner(): lax.all_to_all(blocks, axis, split_axis=0, concat_axis=0, tiled=True)]
    reduce_sum x21 -> x0, other arithmetic: 15.7 us -> none  [the longest x15 14.8 us: accumulate(): item.reshape(rows_here, cols // PIX, PIX).sum(axis=2)]
  transfers between devices with their start and end apart: 14 -> 0, of which waited for: 14 -> 0; matrix products, arithmetic and copies ran while one was open for 2% -> 0% of each run, Pallas kernels for 0% -> 0%
where the time goes in v1:
time: 97.3 us; the launch traced here: 96.9 us
  Pallas kernels  88.7 us (91%)
  local copies, waits for them, and re-layouts  7.58 us (8%)
    pallas_call x1, Pallas kernels, fit(): pl.pallas_call(kernel, out_shape=jax.ShapeDtypeStruct((NDEV, LANES), F32)...  80.8 us
    pallas_call x1, Pallas kernels, residual(): pl.pallas_call(kernel, grid=(cols // wide,), out_shape=(small, small, jax...  7.9 us
    unnamed x16, local copies, waits for them, and re-layouts  7.58 us

profile of v1, /device:TPU:1, one launch (start us, length us, event | category | flops | bytes accessed | tf_op | source)
XLA Modules:
  0.0 96.9 jit_solution(9158506166673845748)
XLA Ops:
  0.6 0.0 copy-start
  0.6 2.5 %copy-done = bf16[5,128,4096]{2,1,0:T(8,128)(2,1)S(1)} copy-done((bf16[5,128,4096]{2,1,0:T(8,128)(2,1)S(1)}, bf16[5,128,4096]{2,1,0:T(8,128)(2,1)}, u32[]{:S(2)}) %copy-start) | copy-done | bytes 5242904
  3.1 0.0 copy-start.1
  3.1 1.0 %copy-done.1 = bf16[256,768]{1,0:T(8,128)(2,1)S(1)} copy-done((bf16[256,768]{1,0:T(8,128)(2,1)S(1)}, bf16[256,768]{1,0:T(8,128)(2,1)}, u32[]{:S(2)}) %copy-start.1) | copy-done | bytes 393240
  4.1 0.0 copy-start.2
  4.1 0.7 copy-done.2
  4.8 0.0 copy-start.3
  4.8 0.7 copy-done.3
  5.5 0.0 copy-start.4
  5.5 0.7 copy-done.4
  6.2 0.0 copy-start.5
  6.2 0.7 copy-done.5
  6.9 0.0 copy-start.6
  6.9 0.7 copy-done.6
  7.6 0.0 copy-start.7
  7.6 0.7 copy-done.7
  8.2 80.8 %fit.1.coef = f32[128,128]{1,0:T(8,128)S(1)} custom-call(s32[5,24]{1,0:T(8,128)S(1)} %copy-done.3, f32[20]{0:T(128)S(1)} %copy-done.7, s32[1,512]{1,0:T(1,128)S(1)} %bitcast.1, f32[5,512]{1,0:T(8,128)S(1)} %copy-done.2, f32[4,11]{1,0:T(4,128)S(1)} %copy-done.5, f32[4,11]{1,0:T(4,128)S(1)} %copy-done.6, bf16[256,768]{1,0:T(8,128)(2,1)S(1)} %copy-done.1, ...), custom_call_target="tpu_custom_call" | custom-call | tf_op jit(solution)/shard_map/fit/pallas_call | solution.py:335
  89.0 7.9 %residual.1 = (f32[4,11]{1,0:T(4,128)}, f32[4,11]{1,0:T(4,128)}, bf16[5,128,4096]{2,1,0:T(8,128)(2,1)}) custom-call(s32[5,24]{1,0:T(8,128)S(1)} %copy-done.3, f32[20]{0:T(128)S(1)} %copy-done.7, s32[1,512]{1,0:T(1,128)S(1)} %bitcast.2, f32[5,512]{1,0:T(8,128)S(1)} %copy-done.2, f32[128,128]{1,0:T(8,128)S(1)} %fit.1.coef, bf16[5,128,4096]{2,1,0:T(8,128)(2,1)S(1)} %copy-done), custom_call_target="tpu_custom_call" | custom-call | tf_op jit(solution)/shard_map/residual/pallas_call | solution.py:451
Async XLA Ops:
  0.6 2.5 %copy-start = (bf16[5,128,4096]{2,1,0:T(8,128)(2,1)S(1)}, bf16[5,128,4096]{2,1,0:T(8,128)(2,1)}, u32[]{:S(2)}) copy-start(bf16[5,128,4096]{2,1,0:T(8,128)(2,1)} %frames.1) | copy-start | bytes 15728644
  3.1 1.0 %copy-start.1 = (bf16[256,768]{1,0:T(8,128)(2,1)S(1)}, bf16[256,768]{1,0:T(8,128)(2,1)}, u32[]{:S(2)}) copy-start(bf16[256,768]{1,0:T(8,128)(2,1)} %constant.12.link_hbm) | copy-start | bytes 1179652
  4.1 0.7 copy-start.2
  4.8 0.7 copy-start.3
  5.5 0.7 copy-start.4
  6.2 0.7 copy-start.5
  6.9 0.7 copy-start.6
  7.6 0.7 copy-start.7

commit v2 on v1

--- a/solution.py
+++ b/solution.py
@@ -1,4 +1,5 @@
 import functools
+import itertools
 import math
 
 import jax
@@ -100,43 +101,69 @@
     return out
 
 
+def offsets():
+    every = itertools.product(range(PLANES), range(4), range(2), range(4))
+    hops = lambda o: sum(min(o[i], 4 - o[i]) for i in (0, 1, 3))
+    return sorted((o for o in every if any(o)), key=lambda o: (-hops(o), o[2]))
+
+
 def fit_kernel(
     lamps, lines, bundles, nrow,
-    starts, bundle_width, fiber_bundle, amplitude, trace, width, link_hbm, frames_hbm,
-    out,
-    frames, ft, fq, a2, invb, mix, litc, px, tb, xq, whi, wlo, link, row, ag, mom, rs,
-    in_sem, link_sem, ag_send, ag_recv, rs_send, rs_recv,
+    starts_hbm, bundle_hbm, fiber_hbm, amp_hbm, trace_hbm, width_hbm, link_hbm, frames_hbm,
+    out, rates, litc, flags, ptab,
+    starts, bundle_width, fiber_bundle, amplitude, trace, width,
+    frames, ft, fq, a2, invb, mix, px, tb, xq, whi, wlo, link, row, ag, mom, rs,
+    in_sem, small_sem, link_sem, ag_send, ag_recv, rs_send, rs_recv,
 ):
     my_row, my_fib = lax.axis_index("rows"), lax.axis_index("fib")
     me = my_row * 4 + my_fib
-    my_z, my_in = me // PER, me % PER
+    my_z, my_y, my_core = my_row // 8, (my_row // 2) % 4, my_row % 2
     first = my_row * LANES
-
+    zs = [(my_z + i) % PLANES for i in range(PLANES)]
+    ys = [(my_y + i) % 4 for i in range(4)]
+    cores = [my_core, 1 - my_core]
+    fibs = [(my_fib + i) % 4 for i in range(4)]
+    inner = {(y, c): ys[y] * 2 + cores[c] for y in range(4) for c in range(2)}
+    rows_of = {(z, y, c): zs[z] * 8 + inner[y, c] for z in range(PLANES) for y, c in inner}
+
+    barrier = pltpu.get_barrier_semaphore()
+    for off in offsets():
+        peer = (rows_of[off[:3]], fibs[off[3]])
+        pl.semaphore_signal(barrier, inc=1, device_id=peer, device_id_type=MESH)
+
+    small = [
+        pltpu.make_async_copy(a, b, small_sem.at[i])
+        for i, (a, b) in enumerate(
+            (
+                (trace_hbm, trace),
+                (width_hbm, width),
+                (starts_hbm, starts),
+                (bundle_hbm, bundle_width),
+                (fiber_hbm, fiber_bundle),
+                (amp_hbm, amplitude),
+            )
+        )
+    ]
+    for copy in small:
+        copy.start()
     for lamp in range(lamps):
         pltpu.make_async_copy(frames_hbm.at[lamp], frames.at[lamp], in_sem.at[lamp]).start()
     pltpu.make_async_copy(link_hbm, link, link_sem).start()
 
-    barrier = pltpu.get_barrier_semaphore()
-
-    @pl.loop(1, NDEV)
-    def _(i):
-        peer = (me + i) % NDEV
-        pl.semaphore_signal(barrier, inc=1, device_id=(peer // 4, peer % 4), device_id_type=MESH)
-
     def tell_everyone(step):
-        pltpu.make_async_copy(row.at[step], ag.at[step, me], ag_recv.at[step, my_z]).start()
-
-        @pl.loop(1, NDEV)
-        def _(i):
-            peer = (me + i) % NDEV
+        for off in offsets():
             pltpu.make_async_remote_copy(
                 src_ref=row.at[step],
                 dst_ref=ag.at[step, me],
                 send_sem=ag_send.at[step],
                 recv_sem=ag_recv.at[step, my_z],
-                device_id=(peer // 4, peer % 4),
+                device_id=(rows_of[off[:3]], fibs[off[3]]),
                 device_id_type=MESH,
             ).start()
+        pltpu.make_async_copy(row.at[step], ag.at[step, me], ag_recv.at[step, my_z]).start()
+
+    for copy in small:
+        copy.wait()
 
     row[0] = jnp.zeros((1, LANES), F32)
     for j in range(MINE):
@@ -174,6 +201,19 @@
             tb[rows, 0:LANES] = high
             tb[rows, LANES : 2 * LANES] = low
 
+    @pl.loop(0, LANES // 16)
+    def _(b):
+        lane = iota((16, LANES), 1)
+        polys = legendre(t_of(first + b * 16 + iota((16, LANES), 0), nrow), K)
+        for part in range(2):
+            table = jnp.zeros((16, LANES), F32)
+            for k in range(K):
+                table = jnp.where(lane % SLOT == k + part * K, (1.0, -1.0)[part] * polys[k], table)
+            high = table.astype(BF16).astype(F32)
+            table = jnp.where(lane < 2 * SLOT, high, jnp.where(lane < 3 * SLOT, table - high, 0.0))
+            rows = pl.ds(pl.multiple_of(part * LANES + b * 16, 16), 16)
+            ptab[rows, :] = table.astype(BF16)
+
     pl.semaphore_wait(barrier, NDEV - 1)
     tell_everyone(0)
 
@@ -188,6 +228,8 @@
     for lamp in range(lamps):
         amp = jnp.where(sub8w == lamp, amplitude[lamp : lamp + 1, :], amp)
         lit8 = jnp.where(sub8 == lamp, lits[lamp], lit8)
+    blocks = (iota((LANES, LANES), 0) // 16 == iota((LANES, LANES), 1)).astype(F32)
+    flags[...] = jnp.dot(lit8, blocks, preferred_element_type=F32).astype(jnp.int32)
     left = jnp.where(sub8w == lamps, KAPPA / base, amp * amp)
     right = jnp.concatenate([lit8, jnp.where(sub8 == lamps, 1.0, jnp.zeros((8, LANES), F32))], axis=1)
     mixed = lax.dot_general(
@@ -201,10 +243,13 @@
     for lamp in range(lamps):
         pltpu.make_async_copy(frames_hbm.at[lamp], frames.at[lamp], in_sem.at[lamp]).wait()
     spread = iota((8, LANES), 1) // PIX
+    rate = jnp.where(sub8w == lamps, KAPPA / base, amp)
     for b in range(32):
         cols = pl.ds(b * LANES, LANES)
         part = lax.slice_in_dim(amp, (b // 8) * LANES, (b // 8 + 1) * LANES, axis=1)
         bright = jnp.take_along_axis(part, spread + 16 * (b % 8), axis=1)
+        part = lax.slice_in_dim(rate, (b // 8) * LANES, (b // 8 + 1) * LANES, axis=1)
+        rates[:, cols] = jnp.take_along_axis(part, spread + 16 * (b % 8), axis=1)
         total = jnp.zeros((LANES, LANES), F32)
         for lamp in range(lamps):
             weight = litc[lamp] * bright[lamp : lamp + 1, :]
@@ -218,7 +263,7 @@
     pltpu.make_async_copy(link_hbm, link, link_sem).wait()
 
     def one_plane(step, hop):
-        z = (my_z + hop) % PLANES
+        z = zs[hop]
         d0 = pl.multiple_of(z * PER, PER)
         here = ag.at[step, pl.ds(d0, PER)]
         pltpu.make_async_copy(here, here, ag_recv.at[step, z]).wait()
@@ -263,25 +308,27 @@
         for j in range(MINE):
             mom[step, pl.ds(d0, PER), j, :] = moments[j * PER : (j + 1) * PER, :]
 
-        @pl.loop(1 if hop == 0 else 0, PER)
-        def _(i):
-            peer = d0 + (my_in + i) % PER
-            pltpu.make_async_remote_copy(
-                src_ref=mom.at[step, peer],
-                dst_ref=rs.at[step, me],
-                send_sem=rs_send.at[step],
-                recv_sem=rs_recv.at[step],
-                device_id=(peer // 4, peer % 4),
-                device_id_type=MESH,
-            ).start()
-
+        for off in offsets():
+            if off[0] == hop:
+                peer = (rows_of[off[:3]], fibs[off[3]])
+                pltpu.make_async_remote_copy(
+                    src_ref=mom.at[step, peer[0] * 4 + peer[1]],
+                    dst_ref=rs.at[step, me],
+                    send_sem=rs_send.at[step],
+                    recv_sem=rs_recv.at[step, my_z],
+                    device_id=peer,
+                    device_id_type=MESH,
+                ).start()
         if hop == 0:
-            pltpu.make_async_copy(mom.at[step, me], rs.at[step, me], rs_recv.at[step]).start()
+            pltpu.make_async_copy(mom.at[step, me], rs.at[step, me], rs_recv.at[step, my_z]).start()
 
     def solve(step):
-        pltpu.make_async_copy(rs.at[step], rs.at[step], rs_recv.at[step]).wait()
-        parts = [rs[step, pl.ds(32 * i, 32)].sum(axis=0) for i in range(4)]
-        total = (parts[0] + parts[1]) + (parts[2] + parts[3])
+        total = jnp.zeros((MINE, LANES), F32)
+        for hop in (0, 1, 3, 2):
+            d0 = pl.multiple_of(zs[hop] * PER, PER)
+            here = rs.at[step, pl.ds(d0, PER)]
+            pltpu.make_async_copy(here, here, rs_recv.at[step, zs[hop]]).wait()
+            total = total + rs[step, pl.ds(d0, PER)].sum(axis=0)
         high = total.astype(BF16).astype(F32)
         both = jnp.concatenate([high, total - high], axis=0)
         lhs = jnp.concatenate([both, both], axis=1).astype(BF16)
@@ -328,23 +375,35 @@
 def fit(starts, bundle_width, fiber_bundle, amplitude, trace, width, frames, nrow):
     lamps, rows, cols = frames.shape
     vmem = pl.BlockSpec(memory_space=pltpu.VMEM)
-    smem = pl.BlockSpec(memory_space=pltpu.SMEM)
-    hbm = pl.BlockSpec(memory_space=pl.ANY)
+    hbm = pl.BlockSpec(memory_space=pltpu.HBM)
     dma = pltpu.SemaphoreType.DMA
+    like = lambda space, x: space(x.shape, x.dtype)
     kernel = functools.partial(fit_kernel, lamps, starts.shape[1], bundle_width.shape[0], nrow)
+    shape = jax.ShapeDtypeStruct
     return pl.pallas_call(
         kernel,
-        out_shape=jax.ShapeDtypeStruct((NDEV, LANES), F32),
-        in_specs=[smem, smem, vmem, vmem, vmem, vmem, hbm, hbm],
-        out_specs=vmem,
+        out_shape=(
+            shape((NDEV, LANES), F32),
+            shape((8, cols), F32),
+            shape((lamps, LANES, LANES), F32),
+            shape((8, LANES), jnp.int32),
+            shape((2 * LANES, LANES), BF16),
+        ),
+        in_specs=[hbm] * 8,
+        out_specs=(vmem,) * 5,
         scratch_shapes=[
+            like(pltpu.SMEM, starts),
+            like(pltpu.SMEM, bundle_width),
+            like(pltpu.VMEM, fiber_bundle),
+            like(pltpu.VMEM, amplitude),
+            like(pltpu.VMEM, trace),
+            like(pltpu.VMEM, width),
             pltpu.VMEM((lamps, rows, cols), BF16),
             pltpu.VMEM((cols, LANES), F32),
             pltpu.VMEM((32, NDEV, LANES), F32),
             pltpu.VMEM((MINE, NDEV, LANES), F32),
             pltpu.VMEM((MINE, NDEV, LANES), F32),
             pltpu.VMEM((MINE * NDEV, LANES), F32),
-            pltpu.VMEM((lamps, LANES, LANES), F32),
             pltpu.VMEM((2 * LANES, 8 * LANES), BF16),
             pltpu.VMEM((5 * LANES, 2 * LANES), BF16),
             pltpu.VMEM((PER, 8 * LANES), F32),
@@ -356,120 +415,133 @@
             pltpu.VMEM((ITERS, NDEV, MINE, LANES), F32),
             pltpu.VMEM((ITERS, NDEV, MINE, LANES), F32),
             dma((lamps,)),
+            dma((6,)),
             dma,
             dma((ITERS + 1,)),
             dma((ITERS + 1, PLANES)),
             dma((ITERS,)),
-            dma((ITERS,)),
+            dma((ITERS, PLANES)),
         ],
         compiler_params=pltpu.CompilerParams(
-            collective_id=0, has_side_effects=True, vmem_limit_bytes=40 << 20
+            collective_id=0, has_side_effects=True, vmem_limit_bytes=24 << 20
         ),
         name="fit",
-    )(starts, bundle_width, fiber_bundle, amplitude, trace, width, link_table(), frames)
+    )(
+        *(
+            pltpu.with_memory_space_constraint(x, pltpu.HBM)
+            for x in (starts, bundle_width, fiber_bundle, amplitude, trace, width, link_table(), frames)
+        )
+    )
+
+
+BLOCK = 16
 
 
 def residual_kernel(
-    lamps, lines, bundles, nrow,
-    starts, bundle_width, fiber_bundle, amplitude, coef, frames,
+    lamps,
+    flags, coef, rates, litc, ptab, frames,
     trace_out, width_out, out,
-    table, rates, litc, ptab,
+    table, xq, shape, done, sem,
 ):
-    my_row = lax.axis_index("rows")
-    me = my_row * 4 + lax.axis_index("fib")
-    first = my_row * LANES
-    step = pl.program_id(0)
-    wide = frames.shape[2]
-
-    @pl.when(step == 0)
-    def _():
-        mine = coef[pl.ds(me, 1), :]
+    me = lax.axis_index("rows") * 4 + lax.axis_index("fib")
+    blocks = frames.shape[1] // BLOCK
+    cols = frames.shape[2]
+
+    def at(b):
+        return pl.ds(pl.multiple_of(b * BLOCK, BLOCK), BLOCK)
+
+    @pl.loop(0, blocks)
+    def _(b):
+        for lamp in range(lamps):
+
+            @pl.when(flags[lamp, b] == 0)
+            def _():
+                pltpu.make_async_copy(frames.at[lamp, at(b)], out.at[lamp, at(b)], sem).start()
+
+    mine = coef[pl.ds(me, 1), :]
+    for j in range(MINE):
+        trace_out[j : j + 1, :] = mine[:, SLOT * j : SLOT * j + K]
+        width_out[j : j + 1, :] = mine[:, SLOT * j + K : SLOT * j + 2 * K]
+
+    turned = jnp.transpose(coef[...])
+    lane = iota((SLOT, LANES), 1)
+    table[3 * SLOT : 4 * SLOT, :] = jnp.zeros((SLOT, cols), BF16)
+    for fb in range(4):
+        pick = 32 * fb + lane // MINE
+        named = jnp.zeros((SLOT, LANES), F32)
         for j in range(MINE):
-            trace_out[j : j + 1, :] = mine[:, SLOT * j : SLOT * j + K]
-            width_out[j : j + 1, :] = mine[:, SLOT * j + K : SLOT * j + 2 * K]
-        for lamp in range(lamps):
-            litc[lamp] = jnp.transpose(
-                jnp.broadcast_to(lit_row(starts, lamp, lines, first), (LANES, LANES))
-            )
-        lane = iota((LANES, LANES), 1)
-        polys = legendre(t_of(first + iota((LANES, LANES), 0), nrow), K)
-        for part in range(2):
-            tab = jnp.zeros((LANES, LANES), F32)
-            for k in range(K):
-                tab = jnp.where(lane % SLOT == k + part * K, (1.0, -1.0)[part] * polys[k], tab)
-            high = tab.astype(BF16).astype(F32)
-            tab = jnp.where(lane < 2 * SLOT, high, jnp.where(lane < 3 * SLOT, tab - high, 0.0))
-            ptab[pl.ds(part * LANES, LANES), :] = tab.astype(BF16)
-        base = base_row(fiber_bundle[...], bundle_width, bundles)
-        fibers = fiber_bundle.shape[1]
-        sub8w = iota((8, fibers), 0)
-        rate = jnp.broadcast_to(KAPPA / base, (8, fibers))
-        for lamp in range(lamps):
-            rate = jnp.where(sub8w == lamp, amplitude[lamp : lamp + 1, :], rate)
-        turned = jnp.transpose(coef[...])
-        lane = iota((SLOT, LANES), 1)
-        lane8 = iota((8, LANES), 1) // PIX
-        for fb in range(4):
-            pick = 32 * fb + lane // MINE
-            named = jnp.zeros((SLOT, LANES), F32)
-            for j in range(MINE):
-                got = jnp.take_along_axis(turned[SLOT * j : SLOT * (j + 1), :], pick, axis=1)
-                named = jnp.where(lane % MINE == j, got, named)
-            part = rate[:, fb * LANES : (fb + 1) * LANES]
-            for b in range(8):
-                cols = pl.ds((8 * fb + b) * LANES, LANES)
-                got = jnp.take_along_axis(named, lane // PIX + 16 * b, axis=1)
-                high, low = split(got)
-                table[0:SLOT, cols] = high
-                table[SLOT : 2 * SLOT, cols] = low
-                table[2 * SLOT : 3 * SLOT, cols] = high
-                table[3 * SLOT : 4 * SLOT, cols] = jnp.zeros((SLOT, LANES), BF16)
-                rates[:, cols] = jnp.take_along_axis(part, lane8 + 16 * b, axis=1)
+            got = jnp.take_along_axis(turned[SLOT * j : SLOT * (j + 1), :], pick, axis=1)
+            named = jnp.where(lane % MINE == j, got, named)
+        for b in range(8):
+            here = pl.ds((8 * fb + b) * LANES, LANES)
+            got = jnp.take_along_axis(named, lane // PIX + 16 * b, axis=1)
+            high, low = split(got)
+            table[0:SLOT, here] = high
+            table[SLOT : 2 * SLOT, here] = low
+            table[2 * SLOT : 3 * SLOT, here] = high
+    xq[...] = jnp.dot(ptab[...], table[...], preferred_element_type=F32)
 
     offset = (iota((1, LANES), 1) % PIX).astype(F32) - (PIX - 1) / 2.0
-    here = pl.ds(pl.multiple_of(step * wide, LANES), wide)
-    xq = jnp.dot(ptab[...], table[:, here], preferred_element_type=F32)
-    rate = rates[:, here]
-    for b in range(wide // LANES):
-        cols = slice(b * LANES, (b + 1) * LANES)
-        x, q = xq[0:LANES, cols], xq[LANES : 2 * LANES, cols]
-        u = (offset - x) * (jnp.exp(q) * rate[lamps : lamps + 1, cols])
-        g = jnp.exp2(-(u * u))
-        for lamp in range(lamps):
-            model = (litc[lamp] * rate[lamp : lamp + 1, cols]) * g
-            out[lamp, :, cols] = (frames[lamp, :, cols].astype(F32) - model).astype(BF16)
-
-
-def residual(starts, bundle_width, fiber_bundle, amplitude, coef, frames, nrow):
+
+    @pl.loop(0, blocks)
+    def _(b):
+        lit = flags[0, b]
+        for lamp in range(1, lamps):
+            lit = lit + flags[lamp, b]
+
+        @pl.when(lit > 0)
+        def _():
+            for i in range(cols // LANES):
+                here = slice(i * LANES, (i + 1) * LANES)
+                x = xq[at(b), here]
+                q = xq[pl.ds(pl.multiple_of(LANES + b * BLOCK, BLOCK), BLOCK), here]
+                u = (offset - x) * (jnp.exp(q) * rates[lamps : lamps + 1, here])
+                shape[:, here] = jnp.exp2(-(u * u))
+            for lamp in range(lamps):
+
+                @pl.when(flags[lamp, b] > 0)
+                def _():
+                    column = litc[lamp, at(b), :]
+                    for i in range(cols // LANES):
+                        here = slice(i * LANES, (i + 1) * LANES)
+                        model = (column * rates[lamp : lamp + 1, here]) * shape[:, here]
+                        seen = frames[lamp, at(b), here].astype(F32)
+                        done[lamp, at(b), here] = (seen - model).astype(BF16)
+                    pltpu.make_async_copy(done.at[lamp, at(b)], out.at[lamp, at(b)], sem).start()
+
+    pltpu.make_async_copy(frames, out, sem).wait()
+
+
+def residual(flags, coef, rates, litc, ptab, frames):
     lamps, rows, cols = frames.shape
-    wide = 512
     vmem = pl.BlockSpec(memory_space=pltpu.VMEM)
     smem = pl.BlockSpec(memory_space=pltpu.SMEM)
-    strip = pl.BlockSpec((lamps, rows, wide), lambda i: (0, 0, i))
-    kernel = functools.partial(residual_kernel, lamps, starts.shape[1], bundle_width.shape[0], nrow)
+    hbm = pl.BlockSpec(memory_space=pltpu.HBM)
     small = jax.ShapeDtypeStruct((MINE, K), F32)
     return pl.pallas_call(
-        kernel,
-        grid=(cols // wide,),
+        functools.partial(residual_kernel, lamps),
         out_shape=(small, small, jax.ShapeDtypeStruct(frames.shape, BF16)),
-        in_specs=[smem, smem, vmem, vmem, vmem, strip],
-        out_specs=(vmem, vmem, strip),
+        in_specs=[smem, vmem, vmem, vmem, vmem, vmem],
+        out_specs=(vmem, vmem, hbm),
         scratch_shapes=[
             pltpu.VMEM((LANES, cols), BF16),
-            pltpu.VMEM((8, cols), F32),
-            pltpu.VMEM((lamps, LANES, LANES), F32),
-            pltpu.VMEM((2 * LANES, LANES), BF16),
+            pltpu.VMEM((2 * LANES, cols), F32),
+            pltpu.VMEM((BLOCK, cols), F32),
+            pltpu.VMEM((lamps, rows, cols), BF16),
+            pltpu.SemaphoreType.DMA,
         ],
-        compiler_params=pltpu.CompilerParams(vmem_limit_bytes=30 << 20),
+        compiler_params=pltpu.CompilerParams(vmem_limit_bytes=24 << 20),
         name="residual",
-    )(starts, bundle_width, fiber_bundle, amplitude, coef, frames)
+    )(flags, coef, rates, litc, ptab, frames)
 
 
 def body(frames, amplitude, line_start, bundle_width, fiber_bundle, trace_coef, width_coef):
     nrow = frames.shape[1] * lax.axis_size("rows")
     bundle = fiber_bundle.reshape(1, -1)
-    coef = fit(line_start, bundle_width, bundle, amplitude, trace_coef, width_coef, frames, nrow)
-    return residual(line_start, bundle_width, bundle, amplitude, coef, frames, nrow)
+    coef, rates, litc, flags, ptab = fit(
+        line_start, bundle_width, bundle, amplitude, trace_coef, width_coef, frames, nrow
+    )
+    return residual(flags, coef, rates, litc, ptab, frames)
 
 
 def solution(mesh):

time: 97.3 us -> 71.1 us (0.73)
  Pallas kernels: 88.7 us -> 70.5 us
  local copies, waits for them, and re-layouts: 7.58 us -> 0.01 us
    pallas_call x2, Pallas kernels: 88.7 us -> 70.5 us  [the longest x1 66.4 us: fit(): pl.pallas_call(kernel, out_shape=(shape((NDEV, LANES), F32), shape((8, co...]
    unnamed x16 -> x2, local copies, waits for them, and re-layouts: 7.58 us -> 0.01 us
where the time goes in v2:
time: 71.1 us
  Pallas kernels  70.5 us (99%)
    pallas_call x1, Pallas kernels, fit(): pl.pallas_call(kernel, out_shape=(shape((NDEV, LANES), F32), shape((8, co...  66.4 us
    pallas_call x1, Pallas kernels, residual(): pl.pallas_call(functools.partial(residual_kernel, lamps), out_shape=(smal...  4.1 us

profile of v2, /device:TPU:1, one launch (start us, length us, event | category | flops | bytes accessed | tf_op | source)
XLA Modules:
  0.0 71.1 jit_solution(6044929665927988170)
XLA Ops:
  0.6 0.0 copy-start
  0.6 66.4 %fit.1 = (f32[128,128]{1,0:T(8,128)S(1)}, f32[8,4096]{1,0:T(8,128)S(1)}, f32[5,128,128]{2,1,0:T(8,128)S(1)}, s32[8,128]{1,0:T(8,128)S(1)}, bf16[256,128]{1,0:T(8,128)(2,1)S(1)}) custom-call(s32[5,24]{1,0:T(8,128)} %starts_hbm.1, f32[20]{0:T(128)} %bundle_hbm.1, s32[1,512]{1,0:T(1,128)} %bitcast.1, f32[5,512]{1,0:T(8,128)} %amp_hbm.1, f32[4,11]{1,0:T(4,128)} %trace_hbm.1, ...), custom_call_target="tpu_custom_call" | custom-call | tf_op jit(solution)/shard_map/fit/pallas_call | solution.py:383
  67.0 0.0 copy-done
  67.0 4.1 %residual.1 = (f32[4,11]{1,0:T(4,128)}, f32[4,11]{1,0:T(4,128)}, bf16[5,128,4096]{2,1,0:T(8,128)(2,1)}) custom-call(s32[8,128]{1,0:T(8,128)S(1)} %get-tuple-element.8.flags, f32[128,128]{1,0:T(8,128)S(1)} %get-tuple-element.9.coef, f32[8,4096]{1,0:T(8,128)S(1)} %get-tuple-element.10.rates, f32[5,128,128]{2,1,0:T(8,128)S(1)} %get-tuple-element.11.litc, ...), custom_call_target="tpu_custom_call" | custom-call | tf_op jit(solution)/shard_map/residual/pallas_call | solution.py:521
Async XLA Ops:
  0.6 66.4 %copy-start = (bf16[5,128,4096]{2,1,0:T(8,128)(2,1)S(1)}, bf16[5,128,4096]{2,1,0:T(8,128)(2,1)}, u32[]{:S(2)}) copy-start(bf16[5,128,4096]{2,1,0:T(8,128)(2,1)} %frames.1) | copy-start | bytes 15728644

commit v3 on v2

--- a/solution.py
+++ b/solution.py
@@ -49,6 +49,7 @@
 
 MOMENTS = 2 * K - 1
 GRAD0 = 3 * MOMENTS
+PACK = GRAD0 + 2 * K
 
 
 def link_table():
@@ -72,12 +73,17 @@
 def legendre(t, count):
     polys = [jnp.ones_like(t), t]
     for n in range(1, count - 1):
-        polys.append(((2 * n + 1) * t * polys[n] - n * polys[n - 1]) / (n + 1))
+        slope = t * ((2 * n + 1) / (n + 1))
+        polys.append(slope * polys[n] - (n / (n + 1)) * polys[n - 1])
     return polys[:count]
 
 
 def t_of(row, total):
     return (2.0 * row.astype(F32) + 1.0) / total - 1.0
+
+
+def pick(x, lanes):
+    return jnp.take_along_axis(x, lanes, axis=1)
 
 
 def split(x):
@@ -112,7 +118,7 @@
     starts_hbm, bundle_hbm, fiber_hbm, amp_hbm, trace_hbm, width_hbm, link_hbm, frames_hbm,
     out, rates, litc, flags, ptab,
     starts, bundle_width, fiber_bundle, amplitude, trace, width,
-    frames, ft, fq, a2, invb, mix, px, tb, xq, whi, wlo, link, row, ag, mom, rs,
+    frames, ft, fq, a2, invb, mix, px, tb, xq, w, link, row, ag, mom, rs,
     in_sem, small_sem, link_sem, ag_send, ag_recv, rs_send, rs_recv,
 ):
     my_row, my_fib = lax.axis_index("rows"), lax.axis_index("fib")
@@ -183,39 +189,45 @@
             px[pl.ds(SLOT * j, SLOT), lanes] = high
             px[pl.ds(LANES + SLOT * j, SLOT), lanes] = low
 
-    @pl.loop(0, LANES // 16)
-    def _(b):
-        lane = iota((16, LANES), 1)
-        degree = jnp.where(lane < GRAD0, lane % MOMENTS, (lane - GRAD0) % K)
-        degree = jnp.where(lane < GRAD0 + 2 * K, degree, -1)
-        wide = legendre(t_of(first + b * 16 + iota((16, LANES), 0), nrow), MOMENTS)
-        table = jnp.zeros((16, LANES), F32)
-        for k in range(MOMENTS):
-            table = jnp.where(degree == k, wide[k], table)
-        table = table * jnp.where(lane < GRAD0, KAPPA**-4, KAPPA**-2)
-        ends = [0, MOMENTS, 2 * MOMENTS, GRAD0, GRAD0 + K, GRAD0 + 2 * K]
-        for a in range(5):
-            inside = (lane >= ends[a]) & (lane < ends[a + 1])
-            high, low = split(jnp.where(inside, table, 0.0))
-            rows = pl.ds(pl.multiple_of(a * LANES + b * 16, 16), 16)
-            tb[rows, 0:LANES] = high
-            tb[rows, LANES : 2 * LANES] = low
-
-    @pl.loop(0, LANES // 16)
-    def _(b):
-        lane = iota((16, LANES), 1)
-        polys = legendre(t_of(first + b * 16 + iota((16, LANES), 0), nrow), K)
+    lane = iota((LANES, LANES), 1)
+    degree = jnp.where(lane < GRAD0, lane % MOMENTS, (lane - GRAD0) % K)
+    degree = jnp.where(lane < GRAD0 + 2 * K, degree, -1)
+    wide = legendre(t_of(first + iota((LANES, LANES), 0), nrow), MOMENTS)
+    table = jnp.zeros((LANES, LANES), F32)
+    for k in range(MOMENTS):
+        table = jnp.where(degree == k, wide[k], table)
+    table = table * jnp.where(lane < GRAD0, KAPPA**-4, KAPPA**-2)
+    ends = [0, MOMENTS, 2 * MOMENTS, GRAD0, GRAD0 + K, GRAD0 + 2 * K]
+    for a in range(5):
+        inside = (lane >= ends[a]) & (lane < ends[a + 1])
+        high, low = split(jnp.where(inside, table, 0.0))
+        for at in (2 * a, 2 * a + 1):
+            tb[at * LANES : (at + 1) * LANES, 0:LANES] = high
+            tb[at * LANES : (at + 1) * LANES, LANES : 2 * LANES] = low
+
+    pl.semaphore_wait(barrier, NDEV - 1)
+    tell_everyone(0)
+
+    def for_residual():
+        lane = iota((LANES, LANES), 1)
+        polys = legendre(t_of(first + iota((LANES, LANES), 0), nrow), K)
         for part in range(2):
-            table = jnp.zeros((16, LANES), F32)
+            table = jnp.zeros((LANES, LANES), F32)
             for k in range(K):
                 table = jnp.where(lane % SLOT == k + part * K, (1.0, -1.0)[part] * polys[k], table)
             high = table.astype(BF16).astype(F32)
             table = jnp.where(lane < 2 * SLOT, high, jnp.where(lane < 3 * SLOT, table - high, 0.0))
-            rows = pl.ds(pl.multiple_of(part * LANES + b * 16, 16), 16)
-            ptab[rows, :] = table.astype(BF16)
-
-    pl.semaphore_wait(barrier, NDEV - 1)
-    tell_everyone(0)
+            ptab[part * LANES : (part + 1) * LANES, :] = table.astype(BF16)
+        base = base_row(fiber_bundle[...], bundle_width, bundles)
+        rate = jnp.broadcast_to(KAPPA / base, (8, amplitude.shape[1]))
+        for lamp in range(lamps):
+            rate = jnp.where(iota(rate.shape, 0) == lamp, amplitude[lamp : lamp + 1, :], rate)
+        spread = iota((8, LANES), 1) // PIX
+        for b in range(32):
+            part = lax.slice_in_dim(rate, (b // 8) * LANES, (b // 8 + 1) * LANES, axis=1)
+            rates[:, b * LANES : (b + 1) * LANES] = jnp.take_along_axis(
+                part, spread + 16 * (b % 8), axis=1
+            )
 
     lits = [lit_row(starts, lamp, lines, first) for lamp in range(lamps)]
     for lamp in range(lamps):
@@ -243,13 +255,10 @@
     for lamp in range(lamps):
         pltpu.make_async_copy(frames_hbm.at[lamp], frames.at[lamp], in_sem.at[lamp]).wait()
     spread = iota((8, LANES), 1) // PIX
-    rate = jnp.where(sub8w == lamps, KAPPA / base, amp)
     for b in range(32):
         cols = pl.ds(b * LANES, LANES)
         part = lax.slice_in_dim(amp, (b // 8) * LANES, (b // 8 + 1) * LANES, axis=1)
         bright = jnp.take_along_axis(part, spread + 16 * (b % 8), axis=1)
-        part = lax.slice_in_dim(rate, (b // 8) * LANES, (b // 8 + 1) * LANES, axis=1)
-        rates[:, cols] = jnp.take_along_axis(part, spread + 16 * (b % 8), axis=1)
         total = jnp.zeros((LANES, LANES), F32)
         for lamp in range(lamps):
             weight = litc[lamp] * bright[lamp : lamp + 1, :]
@@ -260,31 +269,35 @@
     def _(q):
         fq[q] = ft[pl.ds(q, NDEV, stride=32), :]
 
+    for_residual()
     pltpu.make_async_copy(link_hbm, link, link_sem).wait()
 
-    def one_plane(step, hop):
-        z = zs[hop]
-        d0 = pl.multiple_of(z * PER, PER)
-        here = ag.at[step, pl.ds(d0, PER)]
-        pltpu.make_async_copy(here, here, ag_recv.at[step, z]).wait()
-        coef = ag[step, pl.ds(d0, PER), 0, :]
+    def profiles(step, hops, slot):
+        starts_at = [pl.multiple_of(zs[hop] * PER, PER) for hop in hops]
+        for hop, d0 in zip(hops, starts_at):
+            here = ag.at[step, pl.ds(d0, PER)]
+            pltpu.make_async_copy(here, here, ag_recv.at[step, zs[hop]]).wait()
+        coef = jnp.concatenate([ag[step, pl.ds(d0, PER), 0, :] for d0 in starts_at], axis=0)
         high, low = split(coef)
         lhs = jnp.concatenate(
             [jnp.concatenate([high, high], axis=1), jnp.concatenate([low, low], axis=1)], axis=0
         )
         both = jnp.dot(lhs, px[...], preferred_element_type=F32)
-        xq[...] = both[0:PER] + both[PER : 2 * PER]
-
+        xq[slot] = both[0 : 2 * PER] + both[2 * PER : 4 * PER]
+
+    def column_sums(hops, slot):
+        starts_at = [pl.multiple_of(zs[hop] * PER, PER) for hop in hops]
         for j in range(MINE):
-            for half in range(2):
-                rows = pl.ds(half * 16, 16)
-                drows = pl.ds(pl.multiple_of(d0 + half * 16, 16), 16)
-                x = xq[rows, (2 * j) * LANES : (2 * j + 1) * LANES]
-                inv = jnp.exp(xq[rows, (2 * j + 1) * LANES : (2 * j + 2) * LANES]) * invb[j, drows, :]
+            for part in range(4):
+                rows = slice(part * 16, part * 16 + 16)
+                d0 = starts_at[part // 2]
+                drows = pl.ds(pl.multiple_of(d0 + (part % 2) * 16, 16), 16)
+                x = xq[slot, rows, (2 * j) * LANES : (2 * j + 1) * LANES]
+                inv = jnp.exp(xq[slot, rows, (2 * j + 1) * LANES : (2 * j + 2) * LANES]) * invb[j, drows, :]
                 bright2 = a2[j, drows, :]
                 sxx = sxs = sss = hx = hs = jnp.zeros((16, LANES), F32)
+                u = (-(PIX - 1) / 2.0 - x) * inv
                 for p in range(PIX):
-                    u = ((p - (PIX - 1) / 2.0) - x) * inv
                     g = jnp.exp2(-(u * u))
                     gu = g * u
                     m = gu * gu
@@ -295,68 +308,114 @@
                     sss = sss + n * u
                     hx = hx + tg
                     hs = hs + tg * u
-                binv = bright2 * inv
-                sums = (binv * inv * sxx, binv * sxs, bright2 * sss, inv * hx, hs)
-                wrows = pl.ds(j * PER + half * 16, 16)
+                    u = u + inv
+                sums = (bright2 * sxx * inv * inv, bright2 * sxs * inv, bright2 * sss, inv * hx, hs)
+                wrows = slice(j * 2 * PER + part * 16, j * 2 * PER + part * 16 + 16)
                 for a in range(5):
                     h, l = split(sums[a])
-                    whi[wrows, a * LANES : (a + 1) * LANES] = h
-                    wlo[wrows, a * LANES : (a + 1) * LANES] = l
-        one = jnp.dot(whi[...], tb[...], preferred_element_type=F32)
-        two = jnp.dot(wlo[...], tb[:, 0:LANES], preferred_element_type=F32)
-        moments = one[:, 0:LANES] + one[:, LANES : 2 * LANES] + two
-        for j in range(MINE):
-            mom[step, pl.ds(d0, PER), j, :] = moments[j * PER : (j + 1) * PER, :]
-
-        for off in offsets():
-            if off[0] == hop:
-                peer = (rows_of[off[:3]], fibs[off[3]])
-                pltpu.make_async_remote_copy(
-                    src_ref=mom.at[step, peer[0] * 4 + peer[1]],
-                    dst_ref=rs.at[step, me],
-                    send_sem=rs_send.at[step],
-                    recv_sem=rs_recv.at[step, my_z],
-                    device_id=peer,
-                    device_id_type=MESH,
-                ).start()
-        if hop == 0:
-            pltpu.make_async_copy(mom.at[step, me], rs.at[step, me], rs_recv.at[step, my_z]).start()
+                    w[slot, wrows, 2 * a * LANES : (2 * a + 1) * LANES] = h
+                    w[slot, wrows, (2 * a + 1) * LANES : (2 * a + 2) * LANES] = l
+
+    def moments_of(slot):
+        both = jnp.dot(w[slot], tb[...], preferred_element_type=F32)
+        return both[:, 0:LANES] + both[:, LANES : 2 * LANES]
+
+    def send(step, hops, moments):
+        starts_at = [pl.multiple_of(zs[hop] * PER, PER) for hop in hops]
+        lane = iota((PER, LANES), 1)
+        for i, (hop, d0) in enumerate(zip(hops, starts_at)):
+            at = [moments[(2 * j + i) * PER : (2 * j + i + 1) * PER, :] for j in range(MINE)]
+            second = pltpu.roll(at[1], PACK, axis=1)
+            third = pltpu.roll(at[2], LANES - PACK, axis=1)
+            drows = pl.ds(d0, PER)
+            mom[step, drows, 0, :] = jnp.where(lane < PACK, at[0], second)
+            mom[step, drows, 1, :] = jnp.where(lane < 2 * PACK - LANES, second, third)
+            mom[step, drows, 2, :] = at[3]
+            for off in offsets():
+                if off[0] == hop:
+                    peer = (rows_of[off[:3]], fibs[off[3]])
+                    pltpu.make_async_remote_copy(
+                        src_ref=mom.at[step, peer[0] * 4 + peer[1]],
+                        dst_ref=rs.at[step, me],
+                        send_sem=rs_send.at[step],
+                        recv_sem=rs_recv.at[step, my_z],
+                        device_id=peer,
+                        device_id_type=MESH,
+                    ).start()
+            if hop == 0:
+                mine = rs.at[step, me]
+                pltpu.make_async_copy(mom.at[step, me], mine, rs_recv.at[step, my_z]).start()
 
     def solve(step):
-        total = jnp.zeros((MINE, LANES), F32)
-        for hop in (0, 1, 3, 2):
+        total = jnp.zeros((3, LANES), F32)
+        for hop in (2, 1, 3, 0):
             d0 = pl.multiple_of(zs[hop] * PER, PER)
             here = rs.at[step, pl.ds(d0, PER)]
             pltpu.make_async_copy(here, here, rs_recv.at[step, zs[hop]]).wait()
-            total = total + rs[step, pl.ds(d0, PER)].sum(axis=0)
+            parts = [rs[step, pl.ds(d0 + 8 * i, 8)].sum(axis=0) for i in range(4)]
+            total = total + ((parts[0] + parts[1]) + (parts[2] + parts[3]))
+        lane = iota((1, LANES), 1)
+        top, middle, bottom = total[0:1], total[1:2], total[2:3]
+        second = pltpu.roll(jnp.where(lane < PACK, middle, top), LANES - PACK, axis=1)
+        third = pltpu.roll(middle, PACK, axis=1)
+        sub = iota((MINE, LANES), 0)
+        total = jnp.where(
+            sub < 2, jnp.where(sub == 0, top, second), jnp.where(sub == 2, third, bottom)
+        )
         high = total.astype(BF16).astype(F32)
         both = jnp.concatenate([high, total - high], axis=0)
         lhs = jnp.concatenate([both, both], axis=1).astype(BF16)
         both = jnp.dot(lhs, link[...], preferred_element_type=F32)
         both = both[0:MINE] + both[MINE : 2 * MINE]
         lane = iota((MINE, LANES), 1)
+        group, within = lane // SLOT, lane % SLOT
         system = []
-        for i in range(2 * K):
-            block = both[:, (i // 4) * LANES : (i // 4 + 1) * LANES]
-            if i % 4:
-                block = pltpu.roll(block, LANES - SLOT * (i % 4), axis=1)
-            system.append(jnp.where(lane == i, block + 1.0, block))
-        for k in range(2 * K):
-            scaled = system[k] * (1.0 / system[k][:, k : k + 1])
-            for i in range(2 * K):
-                if i != k:
-                    system[i] = system[i] - system[i][:, k : k + 1] * scaled
-            system[k] = scaled
+        for v in range(6):
+            block = both[:, v * LANES : (v + 1) * LANES]
+            system.append(jnp.where(within == 4 * v + group, block + 1.0, block))
+        for v in range(6):
+            width_of = min(4, 2 * K - 4 * v)
+            mine = range(width_of)
+            ahead = [pick(system[v], within + SLOT * g) for g in mine]
+            pivot = [
+                [pick(system[v], jnp.full_like(lane, SLOT * g + 4 * v + b)) for b in mine] for g in mine
+            ]
+            cols = [[pick(x, group * SLOT + 4 * v + b) for b in mine] for x in system]
+            for g in mine:
+                unit = 1.0 / pivot[g][g]
+                ahead[g] = ahead[g] * unit
+                for b in range(g + 1, width_of):
+                    pivot[g][b] = pivot[g][b] * unit
+                for c in mine:
+                    if c != g:
+                        ahead[c] = ahead[c] - pivot[c][g] * ahead[g]
+                        for b in range(g + 1, width_of):
+                            pivot[c][b] = pivot[c][b] - pivot[c][g] * pivot[g][b]
+            for u in range(6):
+                taken = cols[u][0] * ahead[0]
+                for b in range(1, width_of):
+                    taken = taken + cols[u][b] * ahead[b]
+                system[u] = system[u] - taken
+                if u == v:
+                    for g in mine:
+                        system[u] = jnp.where(group == g, ahead[g], system[u])
         found = jnp.zeros((MINE, LANES), F32)
-        for i in range(2 * K):
-            found = jnp.where(lane % SLOT == i, system[i][:, 2 * K : 2 * K + 1], found)
-        found = jnp.where(iota((MINE, LANES), 0) == lane // SLOT, found, 0.0)
+        for v in range(6):
+            got = pick(system[v], (within % 4) * SLOT + 2 * K)
+            found = jnp.where((within // 4 == v) & (within < 2 * K), got, found)
+        found = jnp.where(iota((MINE, LANES), 0) == group, found, 0.0)
         row[step + 1] = row[step] + found.sum(axis=0, keepdims=True)
 
     @pl.loop(0, ITERS)
     def _(step):
-        for hop in (0, 1, 3, 2):
-            one_plane(step, hop)
+        early, late = (2, 1), (3, 0)
+        profiles(step, early, 0)
+        profiles(step, late, 1)
+        column_sums(early, 0)
+        moments = moments_of(0)
+        column_sums(late, 1)
+        send(step, early, moments)
+        send(step, late, moments_of(1))
         solve(step)
         tell_everyone(step + 1)
         sent = mom.at[step, pl.ds(0, NDEV - 1)]
@@ -405,15 +464,14 @@
             pltpu.VMEM((MINE, NDEV, LANES), F32),
             pltpu.VMEM((MINE * NDEV, LANES), F32),
             pltpu.VMEM((2 * LANES, 8 * LANES), BF16),
-            pltpu.VMEM((5 * LANES, 2 * LANES), BF16),
-            pltpu.VMEM((PER, 8 * LANES), F32),
-            pltpu.VMEM((LANES, 5 * LANES), BF16),
-            pltpu.VMEM((LANES, 5 * LANES), BF16),
+            pltpu.VMEM((10 * LANES, 2 * LANES), BF16),
+            pltpu.VMEM((2, 2 * PER, 8 * LANES), F32),
+            pltpu.VMEM((2, 2 * LANES, 10 * LANES), BF16),
             pltpu.VMEM((2 * LANES, 24 * SLOT), BF16),
             pltpu.VMEM((ITERS + 1, 1, LANES), F32),
             pltpu.VMEM((ITERS + 1, NDEV, 1, LANES), F32),
-            pltpu.VMEM((ITERS, NDEV, MINE, LANES), F32),
-            pltpu.VMEM((ITERS, NDEV, MINE, LANES), F32),
+            pltpu.VMEM((ITERS, NDEV, 3, LANES), F32),
+            pltpu.VMEM((ITERS, NDEV, 3, LANES), F32),
             dma((lamps,)),
             dma((6,)),
             dma,

time: 71.1 us -> 65.9 us (0.927)
  Pallas kernels: 70.5 us -> 65.4 us
    pallas_call x1, Pallas kernels: 66.4 us -> 60.9 us  [fit(): pl.pallas_call(kernel, out_shape=(shape((NDEV, LANES), F32), shape((8, co...]
where the time goes in v3:
time: 65.9 us; the launch traced here: 66.1 us
  Pallas kernels  65.4 us (99%)
  between operations  0.66 us (1%)
    pallas_call x1, Pallas kernels, fit(): pl.pallas_call(kernel, out_shape=(shape((NDEV, LANES), F32), shape((8, co...  60.9 us
    pallas_call x1, Pallas kernels, residual(): pl.pallas_call(functools.partial(residual_kernel, lamps), out_shape=(smal...  4.48 us

profile of v3, /device:TPU:1, one launch (start us, length us, event | category | flops | bytes accessed | tf_op | source)
XLA Modules:
  0.0 66.1 jit_solution(5336711319182575181)
XLA Ops:
  0.6 0.0 copy-start
  0.6 60.9 %fit.1 = (f32[128,128]{1,0:T(8,128)S(1)}, f32[8,4096]{1,0:T(8,128)S(1)}, f32[5,128,128]{2,1,0:T(8,128)S(1)}, s32[8,128]{1,0:T(8,128)S(1)}, bf16[256,128]{1,0:T(8,128)(2,1)S(1)}) custom-call(s32[5,24]{1,0:T(8,128)} %starts_hbm.1, f32[20]{0:T(128)} %bundle_hbm.1, s32[1,512]{1,0:T(1,128)} %bitcast.1, f32[5,512]{1,0:T(8,128)} %amp_hbm.1, f32[4,11]{1,0:T(4,128)} %trace_hbm.1, ...), custom_call_target="tpu_custom_call" | custom-call | tf_op jit(solution)/shard_map/fit/pallas_call | solution.py:442
  61.6 0.0 copy-done
  61.6 4.5 %residual.1 = (f32[4,11]{1,0:T(4,128)}, f32[4,11]{1,0:T(4,128)}, bf16[5,128,4096]{2,1,0:T(8,128)(2,1)}) custom-call(s32[8,128]{1,0:T(8,128)S(1)} %get-tuple-element.8.flags, f32[128,128]{1,0:T(8,128)S(1)} %get-tuple-element.9.coef, f32[8,4096]{1,0:T(8,128)S(1)} %get-tuple-element.10.rates, f32[5,128,128]{2,1,0:T(8,128)S(1)} %get-tuple-element.11.litc, ...), custom_call_target="tpu_custom_call" | custom-call | tf_op jit(solution)/shard_map/residual/pallas_call | solution.py:579
Async XLA Ops:
  0.6 61.0 %copy-start = (bf16[5,128,4096]{2,1,0:T(8,128)(2,1)S(1)}, bf16[5,128,4096]{2,1,0:T(8,128)(2,1)}, u32[]{:S(2)}) copy-start(bf16[5,128,4096]{2,1,0:T(8,128)(2,1)} %frames.1) | copy-start | bytes 15728644

commit v4 on v3

--- a/solution.py
+++ b/solution.py
@@ -20,7 +20,7 @@
 PER = 32
 MINE = 4
 SLOT = 32
-KAPPA = math.sqrt(0.5 / math.log(2.0))
+KAPPA = math.sqrt(0.5)
 F32 = jnp.float32
 BF16 = jnp.bfloat16
 MESH = pl.DeviceIdType.MESH
@@ -298,7 +298,7 @@
                 sxx = sxs = sss = hx = hs = jnp.zeros((16, LANES), F32)
                 u = (-(PIX - 1) / 2.0 - x) * inv
                 for p in range(PIX):
-                    g = jnp.exp2(-(u * u))
+                    g = jnp.exp(-(u * u))
                     gu = g * u
                     m = gu * gu
                     n = m * u
@@ -537,8 +537,8 @@
             table[0:SLOT, here] = high
             table[SLOT : 2 * SLOT, here] = low
             table[2 * SLOT : 3 * SLOT, here] = high
-    xq[...] = jnp.dot(ptab[...], table[...], preferred_element_type=F32)
-
+        here = slice(8 * fb * LANES, 8 * (fb + 1) * LANES)
+        xq[:, here] = jnp.dot(ptab[...], table[:, here], preferred_element_type=F32)
     offset = (iota((1, LANES), 1) % PIX).astype(F32) - (PIX - 1) / 2.0
 
     @pl.loop(0, blocks)
@@ -554,7 +554,7 @@
                 x = xq[at(b), here]
                 q = xq[pl.ds(pl.multiple_of(LANES + b * BLOCK, BLOCK), BLOCK), here]
                 u = (offset - x) * (jnp.exp(q) * rates[lamps : lamps + 1, here])
-                shape[:, here] = jnp.exp2(-(u * u))
+                shape[:, here] = jnp.exp(-(u * u))
             for lamp in range(lamps):
 
                 @pl.when(flags[lamp, b] > 0)

time: 65.9 us -> 65.9 us (level)
  no operation moved by 1% of the time
where the time goes in v4:
time: 65.9 us; the launch traced here: 65.7 us
  Pallas kernels  65.1 us (99%)
  between operations  0.66 us (1%)
    pallas_call x1, Pallas kernels, fit(): pl.pallas_call(kernel, out_shape=(shape((NDEV, LANES), F32), shape((8, co...  61 us
    pallas_call x1, Pallas kernels, residual(): pl.pallas_call(functools.partial(residual_kernel, lamps), out_shape=(smal...  4.04 us

profile of v4, /device:TPU:1, one launch (start us, length us, event | category | flops | bytes accessed | tf_op | source)
XLA Modules:
  0.0 65.7 jit_solution(1818202458418733834)
XLA Ops:
  0.6 0.0 copy-start
  0.6 61.0 %fit.1 = (f32[128,128]{1,0:T(8,128)S(1)}, f32[8,4096]{1,0:T(8,128)S(1)}, f32[5,128,128]{2,1,0:T(8,128)S(1)}, s32[8,128]{1,0:T(8,128)S(1)}, bf16[256,128]{1,0:T(8,128)(2,1)S(1)}) custom-call(s32[5,24]{1,0:T(8,128)} %starts_hbm.1, f32[20]{0:T(128)} %bundle_hbm.1, s32[1,512]{1,0:T(1,128)} %bitcast.1, f32[5,512]{1,0:T(8,128)} %amp_hbm.1, f32[4,11]{1,0:T(4,128)} %trace_hbm.1, ...), custom_call_target="tpu_custom_call" | custom-call | tf_op jit(solution)/shard_map/fit/pallas_call | solution.py:442
  61.7 0.0 copy-done
  61.7 4.0 %residual.1 = (f32[4,11]{1,0:T(4,128)}, f32[4,11]{1,0:T(4,128)}, bf16[5,128,4096]{2,1,0:T(8,128)(2,1)}) custom-call(s32[8,128]{1,0:T(8,128)S(1)} %get-tuple-element.8.flags, f32[128,128]{1,0:T(8,128)S(1)} %get-tuple-element.9.coef, f32[8,4096]{1,0:T(8,128)S(1)} %get-tuple-element.10.rates, f32[5,128,128]{2,1,0:T(8,128)S(1)} %get-tuple-element.11.litc, ...), custom_call_target="tpu_custom_call" | custom-call | tf_op jit(solution)/shard_map/residual/pallas_call | solution.py:579
Async XLA Ops:
  0.6 61.0 %copy-start = (bf16[5,128,4096]{2,1,0:T(8,128)(2,1)S(1)}, bf16[5,128,4096]{2,1,0:T(8,128)(2,1)}, u32[]{:S(2)}) copy-start(bf16[5,128,4096]{2,1,0:T(8,128)(2,1)} %frames.1) | copy-start | bytes 15728644
